TPU v7x, 256 devices: a whole 4x4x8 slice. The times are simulated.
256 devices in a mesh: dp: 32 (over y, z), head: 4 (over x), rep: 2 (over core).
Axes of the slice: x: 4, y: 4, z: 8, core: 2. Of those that a mesh axis runs over, the one named last changes fastest.
Arguments:
- embeddings: bfloat16 [16384, 8, 1152], P(('dp', 'head', 'rep')), may hold values from -6 to 6
- coverage: int32 [16384, 2], P(('dp', 'head', 'rep')), may hold values from 0 to 127, all different within a row; in each aligned block of 64 rows (0 to 63, 64 to 127, ...) at most 2 rows name the same one
- labels: int32 [16384, 2, 8], P(('dp', 'head', 'rep')), may hold values 0 or 1
- w_in: bfloat16 [128, 1152, 768], P(('dp', 'head')), may hold values from -0.1875 to 0.1875
- bias_in: bfloat16 [128, 768], P(('dp', 'head')), may hold values from -3 to 3
- w_out: bfloat16 [128, 768], P(('dp', 'head')), may hold values from -0.21875 to 0.21875
- first_w: float32 [128, 1152, 768], P(('dp', 'head'), 'rep'), may hold values from -0.5 to 0.5
- second_w: float32 [128, 1152, 768], P(('dp', 'head'), 'rep'), may hold values from 0.0001 to 0.001
- first_vec: float32 [128, 2, 768], P(('dp', 'head')), may hold values from -0.5 to 0.5
- second_vec: float32 [128, 2, 768], P(('dp', 'head')), may hold values from 0.0001 to 0.01
Outputs:
- new_w_in: bfloat16 [128, 1152, 768], P(('dp', 'head'))
- new_vec: bfloat16 [128, 2, 768], P(('dp', 'head'))
- new_first_w: float32 [128, 1152, 768], P(('dp', 'head'), 'rep')
- new_second_w: float32 [128, 1152, 768], P(('dp', 'head'), 'rep')
- new_first_vec: float32 [128, 2, 768], P(('dp', 'head'))
- new_second_vec: float32 [128, 2, 768], P(('dp', 'head'))
Inputs may be any that keep to these rules, and one draw needn't show every extreme that they name: `coverage`: each block names 2 different heads. Among the 64 blocks of one device (aligned blocks of rows, in order) no head is named more than 2 times, a bound that some block reaches; every head is named by some block.
All inputs are finite; a program needn't handle non-finite values. No bound on the sum of `labels` on one device may be relied on, other than what follows from the above.
Results may differ from a plain program's by a relative error of at most 0.00155.
Values may be sent and summed in bfloat16 or wider, within the bound.
A program may use at most 128 MiB of HBM per device.

v0:
```python
import jax
import jax.numpy as jnp
from jax import lax
from jax.sharding import PartitionSpec as P

beta_one = 0.9
beta_two = 0.999
learn_rate = 0.001
epsilon = 1e-08


def per_device(
    embeddings, coverage, labels, w_in, bias_in, w_out, first_w, second_w, first_vec, second_vec
):
    dp_count = lax.axis_size("dp")
    head_count = lax.axis_size("head")
    owners = dp_count * head_count
    block_count, rows_block, feature = embeddings.shape
    per_block = coverage.shape[1]
    slot_count = 2 * block_count * per_block // owners
    entries = block_count * per_block
    heads_flat = coverage.reshape(entries)
    onehot = (heads_flat[:, None] == jnp.arange(owners, dtype=jnp.int32)[None, :]).astype(jnp.int32)
    slot_rank = jnp.sum((jnp.cumsum(onehot, axis=0) - 1) * onehot, axis=1)
    target_slot = heads_flat * slot_count + slot_rank
    picker = jnp.arange(owners * slot_count, dtype=jnp.int32)[:, None] == target_slot[None, :]
    block_pick = jnp.sum(
        picker.reshape(owners * slot_count, block_count, per_block).astype(jnp.int32), axis=2
    ).astype(jnp.bfloat16)
    send_rows = jnp.dot(
        block_pick,
        embeddings.reshape(block_count, rows_block * feature),
        preferred_element_type=jnp.float32,
    ).astype(jnp.bfloat16)
    label_marks = (labels.reshape(entries, rows_block) + 1).astype(jnp.float32)
    send_marks = jnp.dot(
        picker.astype(jnp.float32), label_marks, precision=lax.Precision.HIGHEST
    ).astype(jnp.bfloat16)
    direct_rows = send_rows.reshape(owners, slot_count, rows_block, feature)
    direct_marks = send_marks.reshape(owners, slot_count, rows_block)
    got_rows, got_marks = (
        lax.all_to_all(direct_rows, ("dp", "head"), split_axis=0, concat_axis=0, tiled=True),
        lax.all_to_all(direct_marks, ("dp", "head"), split_axis=0, concat_axis=0, tiled=True),
    )
    row_data = got_rows.reshape(-1, feature)
    marks_all = got_marks.reshape(-1).astype(jnp.float32)
    usable = marks_all > 0.5
    target = marks_all - 1.0
    out_weight = w_out[0].astype(jnp.float32)
    pre_act = (
        jnp.dot(row_data, w_in[0], preferred_element_type=jnp.float32)
        + bias_in[0].astype(jnp.float32)[None, :]
    )
    sig_pre = jax.nn.sigmoid(pre_act)
    hidden = pre_act * sig_pre
    logits = jnp.sum(hidden * out_weight[None, :], axis=1)
    residual = jnp.where(usable, jax.nn.sigmoid(logits) - target, jnp.zeros_like(logits))
    grad_pre = residual[:, None] * out_weight[None, :] * sig_pre * (1.0 + pre_act * (1.0 - sig_pre))
    grad_low = grad_pre.astype(jnp.bfloat16)
    vec_part = jnp.stack([jnp.sum(grad_pre, axis=0), jnp.sum(residual[:, None] * hidden, axis=0)])
    half_rows = feature // lax.axis_size("rep")
    first_row = lax.axis_index("rep") * half_rows
    full_part = lax.dot_general(
        row_data, grad_low, (((0,), (0,)), ((), ())), preferred_element_type=jnp.float32
    )
    whole_w, grad_vec = lax.psum((full_part, vec_part), "rep")
    grad_w = lax.dynamic_slice_in_dim(whole_w, first_row, half_rows, 0)
    new_first_w = beta_one * first_w[0] + (1.0 - beta_one) * grad_w
    new_second_w = beta_two * second_w[0] + (1.0 - beta_two) * grad_w * grad_w
    old_rows = lax.dynamic_slice_in_dim(w_in[0], first_row, half_rows, 0).astype(jnp.float32)
    new_half = (old_rows - learn_rate * new_first_w / (jnp.sqrt(new_second_w) + epsilon)).astype(
        jnp.bfloat16
    )
    new_w_in = lax.all_gather(new_half, "rep", axis=0, tiled=True)
    vector = jnp.stack([bias_in[0], w_out[0]]).astype(jnp.float32)
    new_first_vec = beta_one * first_vec[0] + (1.0 - beta_one) * grad_vec
    new_second_vec = beta_two * second_vec[0] + (1.0 - beta_two) * grad_vec * grad_vec
    new_vec = (vector - learn_rate * new_first_vec / (jnp.sqrt(new_second_vec) + epsilon)).astype(
        jnp.bfloat16
    )
    return (
        new_w_in[None],
        new_vec[None],
        new_first_w[None],
        new_second_w[None],
        new_first_vec[None],
        new_second_vec[None],
    )


def solution(mesh):
    placed = (
        P(("dp", "head", "rep"), None, None),
        P(("dp", "head", "rep"), None),
        P(("dp", "head", "rep"), None, None),
        P(("dp", "head"), None, None),
        P(("dp", "head"), None),
        P(("dp", "head"), None),
        P(("dp", "head"), "rep", None),
        P(("dp", "head"), "rep", None),
        P(("dp", "head"), None, None),
        P(("dp", "head"), None, None),
    )
    return jax.shard_map(
        per_device,
        mesh=mesh,
        in_specs=placed,
        out_specs=(
            P(("dp", "head"), None, None),
            P(("dp", "head"), None, None),
            P(("dp", "head"), "rep", None),
            P(("dp", "head"), "rep", None),
            P(("dp", "head"), None, None),
            P(("dp", "head"), None, None),
        ),
        check_vma=False,
    )
```

profile of v0, /device:TPU:25, one launch (start us, length us, event | category | flops | bytes accessed | tf_op | source)
XLA Modules:
  0.0 235.1 jit_solution(17417560200644279252)
XLA Ops:
  7.2 0.8 copy.30
  7.9 0.1 eq.36
  8.1 0.1 fusion.10
  8.2 0.2 reduce_window_sum.11
  8.3 0.2 select_reduce_fusion
  8.5 0.7 add_convert_fusion
  9.2 0.1 copy.32
  9.3 0.2 convolution_convert_fusion.1
  9.5 0.8 copy.33
  10.3 15.1 %all-to-all-start.1 = ((bf16[128,2,8]{2,1,0:T(2,128)(2,1)}), bf16[128,2,8]{2,1,0:T(2,128)(2,1)S(1)}, u32[]{:S(2)}, u32[]{:S(2)}) async-start(bf16[128,2,8]{2,1,0:T(2,128)(2,1)} %bitcast.4), calls=%async_computation.1 | async-start | bytes 131072 | tf_op jit(solution)/shard_map/all_to_all | solution.py:43
  25.4 0.1 reduce_sum.48
  25.5 1.5 copy.34
  27.0 0.1 copy.31
  27.1 0.7 multiply_add_fusion
  27.8 0.1 convert_reduce_fusion
  27.9 1.4 convolution_convert_fusion
  29.3 3.1 %copy.35 = bf16[32,8,8,1152]{3,2,1,0:T(8,128)(2,1)} copy(bf16[32,8,8,1152]{3,1,2,0:T(8,128)(2,1)S(1)} %bitcast.56) | data formatting | bytes 9437184
  32.4 1.6 all-to-all-done.1
  34.0 0.0 copy-start.4
  34.0 0.0 copy-start.6
  34.0 0.0 copy-start.3
  34.0 12.2 %all-to-all-start = ((bf16[128,2,8,1152]{3,2,1,0:T(8,128)(2,1)}), bf16[128,2,8,1152]{3,2,1,0:T(8,128)(2,1)}, u32[]{:S(2)}, u32[]{:S(2)}) async-start(bf16[128,2,8,1152]{3,2,1,0:T(8,128)(2,1)} %bitcast.55), calls=%async_computation | async-start | bytes 9437184 | tf_op jit(solution)/shard_map/all_to_all | solution.py:42
  46.2 0.2 all-reduce.2.cloned.1.call-start
  46.4 0.0 copy-done.4
  46.4 0.0 copy-done.6
  46.4 0.1 convert_compare_fusion
  46.5 0.1 gt.15
  46.7 0.1 convert_add_fusion
  46.7 0.2 sub.27
  46.9 101.7 %all-to-all-done = bf16[128,2,8,1152]{3,2,1,0:T(8,128)(2,1)} async-done(((bf16[128,2,8,1152]{3,2,1,0:T(8,128)(2,1)}), bf16[128,2,8,1152]{3,2,1,0:T(8,128)(2,1)}, u32[]{:S(2)}, u32[]{:S(2)}) %all-to-all-start) | async-done | bytes 4718624 | tf_op jit(solution)/shard_map/all_to_all | solution.py:42
  148.6 0.0 copy-done.3
  148.6 7.0 %multiply_reduce_fusion.1 = (f32[2048]{0:T(1024)S(1)}, f32[2048,768]{1,0:T(8,128)S(1)}) fusion(f32[768]{0:T(1024)S(1)} %get-tuple-element.16, f32[768]{0:T(1024)S(1)} %get-tuple-element.17, bf16[2048,1152]{1,0:T(8,128)(2,1)} %bitcast.2, bf16[1,1152,768]{2,1,0:T(8,128)(2,1)S(1)} %copy-done.3), kind=kOutput, calls=%fused_computation.3 | convolution fusion | flops 3634886656 | bytes 12793856 | tf_op jit(solution)/shard_map/dot_general | solution.py:51
  155.7 0.0 copy-start
  155.7 2.6 %copy-done = f32[2048,768]{1,0:T(8,128)} copy-done((f32[2048,768]{1,0:T(8,128)}, f32[2048,768]{1,0:T(8,128)S(1)}, u32[]{:S(2)}) %copy-start) | copy-done | bytes 6291480
  158.3 9.1 %fusion.1 = f32[1152,768]{1,0:T(8,128)} fusion(bf16[2048,1152]{1,0:T(8,128)(2,1)} %bitcast.2, f32[2048,768]{1,0:T(8,128)S(1)} %get-tuple-element.15, f32[2048]{0:T(1024)S(1)} %subtract_select_fusion, f32[768]{0:T(1024)S(1)} %get-tuple-element.16, f32[768]{0:T(1024)S(1)} %get-tuple-element.17), kind=kOutput, calls=%fused_computation.6 | convolution fusion | flops 3641180160 | bytes 14563328 | tf_op jit(solution)/shard_map/dot_general | solution.py:63
  167.4 0.0 copy-start.1
  167.4 0.0 copy-start.2
  167.4 0.0 all-reduce.2.cloned.1.call-update
  167.4 0.0 all-gather.2.cloned.1.call-start
  167.5 36.1 %all-reduce.2.cloned.1.call-done = f32[1152,768]{1,0:T(8,128)} async-done(((f32[1152,768]{1,0:T(8,128)}), f32[1152,768]{1,0:T(8,128)}) %all-reduce.2.cloned.1.call-update) | async-done | bytes 3538960 | tf_op jit(solution)/shard_map/psum | solution.py:66
  203.5 0.0 copy-done.1
  203.5 0.0 copy-done.2
  203.5 4.9 %fusion.8 = (f32[1,576,768]{2,1,0:T(8,128)}, bf16[576,768]{1,0:T(8,128)(2,1)}, f32[1,576,768]{2,1,0:T(8,128)}) fusion(f32[1152,768]{1,0:T(8,128)} %all-reduce.2.cloned.1.call-done, s32[]{:T(128)S(6)} %select_n.12, f32[1,576,768]{2,1,0:T(8,128)S(1)} %copy-done.1, f32[1,576,768]{2,1,0:T(8,128)S(1)} %copy-done.2, bf16[1,1152,768]{2,1,0:T(8,128)(2,1)} %param.13), kind=kLoop, calls=%fused_computation.17 | loop fusion | flops 5750784 | bytes 10616836 | tf_op jit(solution)/shard_map/broadcast_in_dim | solution.py:85
  208.5 0.0 copy-start.5
  208.5 0.0 copy-start.7
  208.5 0.0 copy-start.8
  208.5 0.0 copy-start.9
  208.5 0.0 all-gather.2.cloned.1.call-update
  208.5 5.3 %fusion.16 = (f32[768]{0:T(1024)S(1)}, f32[768]{0:T(1024)S(1)}) fusion(f32[2048,768]{1,0:T(8,128)} %copy-done, f32[768]{0:T(1024)S(1)} %get-tuple-element.17, f32[768]{0:T(1024)S(1)} %get-tuple-element.16, f32[2048]{0:T(1024)S(1)} %subtract_select_fusion), kind=kLoop, calls=%fused_computation.42 | loop fusion | flops 22018560 | bytes 6311936 | tf_op jit(solution)/shard_map/reduce_sum | solution.py:60
  213.9 2.5 %psum.15 = f32[2,768]{1,0:T(2,128)S(1)} all-reduce(f32[2,768]{1,0:T(2,128)S(1)} %pad_maximum_fusion), channel_id=1, replica_groups=mesh['dp'=32,'head'=4,'rep'=2] {'rep'}, use_global_device_ids=true, to_apply=%region_7.8 | all-reduce | flops 1536 | bytes 12288 | tf_op jit(solution)/shard_map/psum | solution.py:66
  216.4 0.0 copy-done.5
  216.4 0.0 copy-done.7
  216.4 0.0 copy-done.8
  216.4 0.0 copy-done.9
  216.4 0.6 fusion.15
  217.0 8.4 %all-gather.2.cloned.1.call-done = bf16[1152,768]{1,0:T(8,128)(2,1)} async-done(((bf16[576,768]{1,0:T(8,128)(2,1)}), bf16[1152,768]{1,0:T(8,128)(2,1)}) %all-gather.2.cloned.1.call-update) | async-done | bytes 1769488 | tf_op jit(solution)/shard_map/all_gather | solution.py:74
  225.4 2.8 %copy.38 = bf16[1,1152,768]{2,1,0:T(8,128)(2,1)} copy(bf16[1,1152,768]{2,1,0:T(8,128)(2,1)} %bitcast.58) | data formatting | bytes 3538944
  (6 shorter events, 0.1 us)
Async XLA Ops:
  10.3 23.7 %all-to-all-start.1 = ((bf16[128,2,8]{2,1,0:T(2,128)(2,1)}), bf16[128,2,8]{2,1,0:T(2,128)(2,1)S(1)}, u32[]{:S(2)}, u32[]{:S(2)}) async-start(bf16[128,2,8]{2,1,0:T(2,128)(2,1)} %bitcast.4), calls=%async_computation.1 | async-start | bytes 131072 | tf_op jit(solution)/shard_map/all_to_all | solution.py:43
  34.0 12.4 %copy-start.4 = (bf16[1,768]{1,0:T(2,128)(2,1)S(1)}, bf16[1,768]{1,0:T(2,128)(2,1)}, u32[]{:S(2)}) copy-start(bf16[1,768]{1,0:T(2,128)(2,1)} %param.15) | copy-start | bytes 4612
  34.0 12.4 %copy-start.6 = (bf16[1,768]{1,0:T(2,128)(2,1)S(1)}, bf16[1,768]{1,0:T(2,128)(2,1)}, u32[]{:S(2)}) copy-start(bf16[1,768]{1,0:T(2,128)(2,1)} %param.14) | copy-start | bytes 4612
  34.0 114.7 %copy-start.3 = (bf16[1,1152,768]{2,1,0:T(8,128)(2,1)S(1)}, bf16[1,1152,768]{2,1,0:T(8,128)(2,1)}, u32[]{:S(2)}) copy-start(bf16[1,1152,768]{2,1,0:T(8,128)(2,1)} %param.13) | copy-start | bytes 5308420
  34.0 114.7 %all-to-all-start = ((bf16[128,2,8,1152]{3,2,1,0:T(8,128)(2,1)}), bf16[128,2,8,1152]{3,2,1,0:T(8,128)(2,1)}, u32[]{:S(2)}, u32[]{:S(2)}) async-start(bf16[128,2,8,1152]{3,2,1,0:T(8,128)(2,1)} %bitcast.55), calls=%async_computation | async-start | bytes 9437184 | tf_op jit(solution)/shard_map/all_to_all | solution.py:42
  46.2 157.4 %all-reduce.2.cloned.1.call-start = ((), (), s32[]{:S(2)}) async-start(), calls=%async_computation.2 | async-start | bytes 7077888 | tf_op jit(solution)/shard_map/psum | solution.py:66
  155.7 2.7 %copy-start = (f32[2048,768]{1,0:T(8,128)}, f32[2048,768]{1,0:T(8,128)S(1)}, u32[]{:S(2)}) copy-start(f32[2048,768]{1,0:T(8,128)S(1)} %get-tuple-element.15) | copy-start | bytes 18874372
  167.4 36.2 %copy-start.1 = (f32[1,576,768]{2,1,0:T(8,128)S(1)}, f32[1,576,768]{2,1,0:T(8,128)}, u32[]{:S(2)}) copy-start(f32[1,576,768]{2,1,0:T(8,128)} %param.17) | copy-start | bytes 5308420
  167.4 36.2 %copy-start.2 = (f32[1,576,768]{2,1,0:T(8,128)S(1)}, f32[1,576,768]{2,1,0:T(8,128)}, u32[]{:S(2)}) copy-start(f32[1,576,768]{2,1,0:T(8,128)} %param.16) | copy-start | bytes 5308420
  167.4 58.0 %all-gather.2.cloned.1.call-start = ((), (), s32[]{:S(2)}) async-start(), calls=%async_computation.3 | async-start | bytes 2654208 | tf_op jit(solution)/shard_map/all_gather | solution.py:74
  208.5 7.9 %copy-start.5 = (bf16[1,768]{1,0:T(2,128)(2,1)S(1)}, bf16[1,768]{1,0:T(2,128)(2,1)}, u32[]{:S(2)}) copy-start(bf16[1,768]{1,0:T(2,128)(2,1)} %param.15) | copy-start | bytes 4612
  208.5 7.9 %copy-start.7 = (bf16[1,768]{1,0:T(2,128)(2,1)S(1)}, bf16[1,768]{1,0:T(2,128)(2,1)}, u32[]{:S(2)}) copy-start(bf16[1,768]{1,0:T(2,128)(2,1)} %param.14) | copy-start | bytes 4612
  208.5 7.9 %copy-start.8 = (f32[1,2,768]{2,1,0:T(2,128)S(1)}, f32[1,2,768]{2,1,0:T(2,128)}, u32[]{:S(2)}) copy-start(f32[1,2,768]{2,1,0:T(2,128)} %param.19) | copy-start | bytes 18436
  208.5 7.9 %copy-start.9 = (f32[1,2,768]{2,1,0:T(2,128)S(1)}, f32[1,2,768]{2,1,0:T(2,128)}, u32[]{:S(2)}) copy-start(f32[1,2,768]{2,1,0:T(2,128)} %param.18) | copy-start | bytes 18436
Sparse Core Ops, SparseCore 0:
  167.5 35.9 all-reduce.1
  208.7 16.7 all-gather.1
where the time goes:
time: 237 us; the launch traced here: 235 us
  waiting for transfers between devices  148 us (62%)
  starting transfers between devices  27.5 us (12%)
  matrix products  17.7 us (7%)
  between operations  14.3 us (6%)
  other arithmetic  13 us (5%)
  local copies, waits for them, and re-layouts  12.3 us (5%)
  blocking collectives  2.51 us (1%)
    all_to_all x1, waiting for transfers between devices, per_device(): lax.all_to_all(direct_rows, ('dp', 'head'), split_axis=0, concat_axis=0,...  102 us
    psum x1, waiting for transfers between devices, per_device(): whole_w, grad_vec = lax.psum((full_part, vec_part), 'rep')  36.1 us
    all_to_all x1, starting transfers between devices, per_device(): lax.all_to_all(direct_marks, ('dp', 'head'), split_axis=0, concat_axis=0,...  15.1 us
    all_to_all x1, starting transfers between devices, per_device(): lax.all_to_all(direct_rows, ('dp', 'head'), split_axis=0, concat_axis=0,...  12.2 us
    unnamed x24, local copies, waits for them, and re-layouts  10.8 us
    dot_general x1, matrix products, per_device(): lax.dot_general(row_data, grad_low, (((0,), (0,)), ((), ())), preferred_e...  9.07 us
    all_gather x1, waiting for transfers between devices, per_device(): new_w_in = lax.all_gather(new_half, 'rep', axis=0, tiled=True)  8.39 us
    dot_general x1, matrix products, per_device(): jnp.dot(row_data, w_in[0], preferred_element_type=jnp.float32)  7 us
  transfers between devices with their start and end apart: 4, of which 4 were waited for; matrix products, arithmetic and copies ran while one was open for 6% of the time, Pallas kernels for 0%

commit v1 on v0

v1 whole, which is shorter than its diff:
```python
import jax
import jax.numpy as jnp
from jax import lax
from jax.experimental import pallas as pl
from jax.experimental.pallas import tpu as pltpu
from jax.sharding import PartitionSpec as P

beta_one = 0.9
beta_two = 0.999
learn_rate = 0.001
epsilon = 1e-08

MESH = pl.DeviceIdType.MESH
NZ = 8
STEP_OF = (0, 1, 3, 5, 7, 6, 4, 2)
CUTS = ((0, 16), (16, 48), (48, 64))
CUTS_AT = {1: 3, 2: 3, 3: 2, 4: 1}
HOP_SIZE = (64, 64, 48, 16)


def plan(coverage, labels, z):
    blocks, top = coverage.shape
    rows = labels.shape[2]
    head = coverage
    plane = (head // 4) % NZ
    spot = (head // 32) * 4 + head % 4
    ahead = (plane - z + NZ) % NZ
    up = ((ahead >= 1) & (ahead <= 3)) | ((ahead == 4) & (spot < 8))
    far_up = jnp.max(jnp.where(up, ahead, 0), axis=1)
    far_down = jnp.max(jnp.where(up | (ahead == 0), 0, NZ - ahead), axis=1)
    number = jnp.arange(blocks, dtype=jnp.int32)

    def place(far):
        first = (far[None, :] > far[:, None]) | (
            (far[None, :] == far[:, None]) & (number[None, :] < number[:, None])
        )
        return jnp.sum(first.astype(jnp.int32), axis=1)

    pos_up, pos_down = place(far_up), place(far_down)
    order = jnp.stack(
        [
            jnp.sum(jnp.where(pos[None, :] == number[:, None], number[None, :], 0), axis=1)
            for pos in (pos_up, pos_down)
        ]
    )
    pos = jnp.where(ahead == 0, number[:, None], jnp.where(up, pos_up[:, None], pos_down[:, None]))
    entries = blocks * top
    flat = head.reshape(entries)
    nth = jnp.arange(entries, dtype=jnp.int32)
    rank = jnp.sum(
        ((flat[None, :] == flat[:, None]) & (nth[None, :] < nth[:, None])).astype(jnp.int32), axis=1
    )
    lane = (plane * 128 + 2 * spot).reshape(entries) + rank
    picker = (lane[:, None] == jnp.arange(NZ * 128, dtype=jnp.int32)[None, :]).astype(jnp.bfloat16)
    facts = jnp.concatenate(
        [
            (labels.reshape(entries, rows) + 1).astype(jnp.bfloat16),
            jnp.broadcast_to(pos.reshape(entries, 1), (entries, 8)).astype(jnp.bfloat16),
        ],
        axis=1,
    )
    table = lax.dot_general(
        facts, picker, (((0,), (0,)), ((), ())), preferred_element_type=jnp.float32
    ).astype(jnp.int32)
    return order, table


def dispatch_kernel(
    order_ref, table_ref, emb_ref, got_ref, marks_ref,
    send_up, send_down, up_1, up_2, up_3, up_4, down_1, down_2, down_3, down_4, picked, facts, places,
    ring_send, ring_recv, fact_send, fact_recv, place_sem, own_sem,
    mark_send, mark_recv, plane_send, plane_recv,
):
    dp, x, core = lax.axis_index("dp"), lax.axis_index("head"), lax.axis_index("rep")
    y, z = dp // NZ, lax.rem(dp, NZ)
    me = y * 4 + x

    def at_plane(z_to):
        return (y * NZ + z_to, x, core)

    def in_plane(j):
        p = lax.rem(me + j, 16)
        return p, ((p // 4) * NZ + z, lax.rem(p, 4), core)

    barrier = pltpu.get_barrier_semaphore()
    for d in range(1, NZ):
        pl.semaphore_signal(
            barrier, inc=1, device_id=at_plane(lax.rem(z + d, NZ)), device_id_type=MESH
        )

    def greet(j, _):
        _, device = in_plane(j)
        pl.semaphore_signal(barrier, inc=1, device_id=device, device_id_type=MESH)
        return 0

    lax.fori_loop(1, 16, greet, 0)

    def arrange(i, _):
        send_up[i] = emb_ref[order_ref[0, i]]
        send_down[i] = emb_ref[order_ref[1, i]]
        return 0

    lax.fori_loop(0, 64, arrange, 0)
    own_facts = pltpu.make_async_copy(
        table_ref.at[:, pl.ds(pl.multiple_of(z * 128, 128), 128)], facts.at[0], own_sem
    )
    own_facts.start()
    own_facts.wait()
    pl.semaphore_wait(barrier, 22)

    fact_copies = []
    for d in range(1, NZ):
        z_to = lax.rem(z + d, NZ)
        copy = pltpu.make_async_remote_copy(
            src_ref=table_ref.at[:, pl.ds(pl.multiple_of(z_to * 128, 128), 128)],
            dst_ref=facts.at[STEP_OF[d]],
            send_sem=fact_send.at[d],
            recv_sem=fact_recv.at[STEP_OF[d]],
            device_id=at_plane(z_to),
            device_id_type=MESH,
        )
        copy.start()
        fact_copies.append(copy)

    rings = (
        (send_up, up_1, up_2, up_3, up_4),
        (send_down, down_1, down_2, down_3, down_4),
    )
    targets = (at_plane(lax.rem(z + 1, NZ)), at_plane(lax.rem(z + NZ - 1, NZ)))
    ring_copies = {}

    def hop(way, number, piece):
        low, high = CUTS[piece]
        copy = pltpu.make_async_remote_copy(
            src_ref=rings[way][number - 1].at[pl.ds(low, high - low)],
            dst_ref=rings[way][number].at[pl.ds(low, high - low)],
            send_sem=ring_send.at[way, number - 1, piece],
            recv_sem=ring_recv.at[way, number - 1, piece],
            device_id=targets[way],
            device_id_type=MESH,
        )
        copy.start()
        ring_copies[way, number, piece] = copy

    for piece in range(3):
        for way in range(2):
            hop(way, 1, piece)

    def load_places(step):
        copy = pltpu.make_async_copy(
            facts.at[step, pl.ds(8, 8)], places.at[step], place_sem.at[step]
        )
        copy.start()
        copy.wait()

    def pick(step, source, low, high):
        def one(q, _):
            picked[step, q] = source[places[step, 0, q]]
            return 0

        lax.fori_loop(low, high, one, 0)

    def spread(step):
        own = pltpu.make_async_copy(
            picked.at[step, pl.ds(2 * me, 2)], got_ref.at[step, me], own_sem
        )
        own.start()

        def send(j, _):
            p, device = in_plane(j)
            pltpu.make_async_remote_copy(
                src_ref=picked.at[step, pl.ds(2 * p, 2)],
                dst_ref=got_ref.at[step, me],
                send_sem=plane_send.at[step],
                recv_sem=plane_recv.at[step],
                device_id=device,
                device_id_type=MESH,
            ).start()
            return 0

        lax.fori_loop(1, 16, send, 0)
        own.wait()

    load_places(0)
    pick(0, emb_ref, 0, 32)
    spread(0)

    for copy in fact_copies:
        copy.wait()
    for step in range(1, NZ):
        load_places(step)

    own_marks = pltpu.make_async_copy(facts.at[:, pl.ds(0, 8)], marks_ref.at[me], own_sem)
    own_marks.start()

    def send_marks(j, _):
        _, device = in_plane(j)
        pltpu.make_async_remote_copy(
            src_ref=facts.at[:, pl.ds(0, 8)],
            dst_ref=marks_ref.at[me],
            send_sem=mark_send,
            recv_sem=mark_recv,
            device_id=device,
            device_id_type=MESH,
        ).start()
        return 0

    lax.fori_loop(1, 16, send_marks, 0)
    own_marks.wait()

    for number in range(1, 5):
        for piece in range(CUTS_AT[number]):
            for way in range(2):
                ring_copies[way, number, piece].wait_recv()
                if number < 4 and piece < CUTS_AT[number + 1]:
                    hop(way, number + 1, piece)
        if number < 4:
            for way in range(2):
                pick(2 * number - 1 + way, rings[way][number], 0, 32)
                spread(2 * number - 1 + way)
        else:
            pick(7, up_4, 0, 16)
            pick(7, down_4, 16, 32)
            spread(7)

    for copy in ring_copies.values():
        copy.wait_send()
    whole = marks_ref.at[pl.ds(0, 15)]
    pltpu.make_async_copy(whole, whole, mark_send).wait()
    pltpu.make_async_copy(whole, whole, mark_recv).wait()
    for step in range(NZ):
        whole = got_ref.at[step, pl.ds(0, 15)]
        pltpu.make_async_copy(whole, whole, plane_send.at[step]).wait()
        pltpu.make_async_copy(whole, whole, plane_recv.at[step]).wait()


def dispatch(order, table, embeddings):
    feature = embeddings.shape[2]
    bf16, i32 = jnp.bfloat16, jnp.int32
    dma = pltpu.SemaphoreType.DMA
    return pl.pallas_call(
        dispatch_kernel,
        out_shape=(
            jax.ShapeDtypeStruct((NZ, 16, 2, 8, feature), bf16),
            jax.ShapeDtypeStruct((16, NZ, 8, 128), i32),
        ),
        in_specs=[
            pl.BlockSpec(memory_space=pltpu.SMEM),
            pl.BlockSpec(memory_space=pltpu.VMEM),
            pl.BlockSpec(memory_space=pltpu.VMEM),
        ],
        out_specs=(
            pl.BlockSpec(memory_space=pltpu.VMEM),
            pl.BlockSpec(memory_space=pltpu.VMEM),
        ),
        scratch_shapes=[
            pltpu.VMEM((64, 8, feature), bf16),
            pltpu.VMEM((64, 8, feature), bf16),
            *[pltpu.VMEM((size, 8, feature), bf16) for size in HOP_SIZE * 2],
            pltpu.VMEM((NZ, 32, 8, feature), bf16),
            pltpu.VMEM((NZ, 16, 128), i32),
            pltpu.SMEM((NZ, 8, 128), i32),
            dma((2, 4, 3)),
            dma((2, 4, 3)),
            dma((NZ,)),
            dma((NZ,)),
            dma((NZ,)),
            dma,
            dma,
            dma,
            dma((NZ,)),
            dma((NZ,)),
        ],
        compiler_params=pltpu.CompilerParams(
            collective_id=0, has_side_effects=True, vmem_limit_bytes=60 << 20
        ),
        name="dispatch",
    )(order, table, embeddings)


def per_device(
    embeddings, coverage, labels, w_in, bias_in, w_out, first_w, second_w, first_vec, second_vec
):
    feature = embeddings.shape[2]
    z = lax.rem(lax.axis_index("dp"), NZ)
    me = (lax.axis_index("dp") // NZ) * 4 + lax.axis_index("head")
    order, table = plan(coverage, labels, z)
    got, marks = dispatch(order, table, embeddings)
    row_data = got.reshape(-1, feature)
    own = lax.dynamic_slice_in_dim(marks, 2 * me, 2, 3)
    marks_all = jnp.transpose(own, (1, 0, 3, 2)).reshape(-1).astype(jnp.float32)
    usable = marks_all > 0.5
    target = marks_all - 1.0
    out_weight = w_out[0].astype(jnp.float32)
    pre_act = (
        jnp.dot(row_data, w_in[0], preferred_element_type=jnp.float32)
        + bias_in[0].astype(jnp.float32)[None, :]
    )
    sig_pre = jax.nn.sigmoid(pre_act)
    hidden = pre_act * sig_pre
    logits = jnp.sum(hidden * out_weight[None, :], axis=1)
    residual = jnp.where(usable, jax.nn.sigmoid(logits) - target, jnp.zeros_like(logits))
    grad_pre = residual[:, None] * out_weight[None, :] * sig_pre * (1.0 + pre_act * (1.0 - sig_pre))
    grad_low = grad_pre.astype(jnp.bfloat16)
    vec_part = jnp.stack([jnp.sum(grad_pre, axis=0), jnp.sum(residual[:, None] * hidden, axis=0)])
    half_rows = feature // lax.axis_size("rep")
    first_row = lax.axis_index("rep") * half_rows
    full_part = lax.dot_general(
        row_data, grad_low, (((0,), (0,)), ((), ())), preferred_element_type=jnp.float32
    )
    whole_w, grad_vec = lax.psum((full_part, vec_part), "rep")
    grad_w = lax.dynamic_slice_in_dim(whole_w, first_row, half_rows, 0)
    new_first_w = beta_one * first_w[0] + (1.0 - beta_one) * grad_w
    new_second_w = beta_two * second_w[0] + (1.0 - beta_two) * grad_w * grad_w
    old_rows = lax.dynamic_slice_in_dim(w_in[0], first_row, half_rows, 0).astype(jnp.float32)
    new_half = (old_rows - learn_rate * new_first_w / (jnp.sqrt(new_second_w) + epsilon)).astype(
        jnp.bfloat16
    )
    new_w_in = lax.all_gather(new_half, "rep", axis=0, tiled=True)
    vector = jnp.stack([bias_in[0], w_out[0]]).astype(jnp.float32)
    new_first_vec = beta_one * first_vec[0] + (1.0 - beta_one) * grad_vec
    new_second_vec = beta_two * second_vec[0] + (1.0 - beta_two) * grad_vec * grad_vec
    new_vec = (vector - learn_rate * new_first_vec / (jnp.sqrt(new_second_vec) + epsilon)).astype(
        jnp.bfloat16
    )
    return (
        new_w_in[None],
        new_vec[None],
        new_first_w[None],
        new_second_w[None],
        new_first_vec[None],
        new_second_vec[None],
    )


def solution(mesh):
    owners = ("dp", "head")
    moments = P(owners, "rep", None)
    vectors = P(owners, None, None)
    everyone = ("dp", "head", "rep")
    placed = (
        P(everyone, None, None),
        P(everyone, None),
        P(everyone, None, None),
        vectors,
        P(owners, None),
        P(owners, None),
        moments,
        moments,
        vectors,
        vectors,
    )
    return jax.shard_map(
        per_device,
        mesh=mesh,
        in_specs=placed,
        out_specs=(vectors, vectors, moments, moments, vectors, vectors),
        check_vma=False,
    )
```

time: 237 us -> 211 us (0.89)
  Pallas kernels: 0 us -> 105 us
  waiting for transfers between devices: 148 us -> 43.8 us
  starting transfers between devices: 27.5 us -> 0.26 us
  other arithmetic: 13 us -> 16.7 us
  local copies, waits for them, and re-layouts: 12.3 us -> 9.1 us
    pallas_call x0 -> x1, Pallas kernels: none -> 105 us  [dispatch(): pl.pallas_call(dispatch_kernel, out_shape=(jax.ShapeDtypeStruct((NZ, 16,...]
    all_to_all x2 -> x0, waiting for transfers between devices: 103 us -> none  [the longest x1 102 us: per_device(): lax.all_to_all(direct_rows, ('dp', 'head'), split_axis=0, concat_axis=0,...]
    all_to_all x2 -> x0, starting transfers between devices: 27.3 us -> none  [the longest x1 15.1 us: per_device(): lax.all_to_all(direct_marks, ('dp', 'head'), split_axis=0, concat_axis=0,...]
    unnamed x24 -> x16, local copies, waits for them, and re-layouts: 10.8 us -> 6.22 us
  transfers between devices with their start and end apart: 4 -> 2, of which waited for: 4 -> 2; matrix products, arithmetic and copies ran while one was open for 6% -> 3% of each run, Pallas kernels for 0% -> 0%
where the time goes in v1:
time: 211 us; the launch traced here: 209 us
  Pallas kernels  105 us (50%)
  waiting for transfers between devices  43.8 us (21%)
  matrix products  17.7 us (8%)
  other arithmetic  16.7 us (8%)
  between operations  14.2 us (7%)
  local copies, waits for them, and re-layouts  9.1 us (4%)
  blocking collectives  2.51 us (1%)
    pallas_call x1, Pallas kernels, dispatch(): pl.pallas_call(dispatch_kernel, out_shape=(jax.ShapeDtypeStruct((NZ, 16,...  105 us
    psum x1, waiting for transfers between devices, per_device(): whole_w, grad_vec = lax.psum((full_part, vec_part), 'rep')  35.4 us
    dot_general x1, matrix products, per_device(): lax.dot_general(row_data, grad_low, (((0,), (0,)), ((), ())), preferred_e...  9.22 us
    all_gather x1, waiting for transfers between devices, per_device(): new_w_in = lax.all_gather(new_half, 'rep', axis=0, tiled=True)  8.41 us
    dot_general x1, matrix products, per_device(): jnp.dot(row_data, w_in[0], preferred_element_type=jnp.float32)  7.54 us
    unnamed x16, local copies, waits for them, and re-layouts  6.22 us
    reduce_sum x1, other arithmetic, per_device(): jnp.sum(grad_pre, axis=0)  5.25 us
    broadcast_in_dim x1, other arithmetic, per_device(): new_second_w[None]  4.95 us
  transfers between devices with their start and end apart: 2, of which 2 were waited for; matrix products, arithmetic and copies ran while one was open for 3% of the time, Pallas kernels for 0%

profile of v1, /device:TPU:25, one launch (start us, length us, event | category | flops | bytes accessed | tf_op | source)
XLA Modules:
  0.0 208.9 jit_solution(12554019075187754294)
XLA Ops:
  7.2 0.0 all-reduce.2.cloned.1.call-start
  7.2 0.7 multiply_add_fusion
  7.9 0.8 copy.36
  8.7 0.2 convert_reduce_fusion.1
  8.9 0.1 select_reduce_fusion.1
  9.0 0.1 select_reduce_fusion
  9.1 0.7 add_convert_fusion
  9.9 0.1 copy.33
  10.0 0.1 convert_element_type.64
  10.1 0.1 copy.32
  10.2 0.1 copy.34
  10.3 0.1 copy.35
  10.4 0.2 reshape.74
  10.6 0.1 eq.42
  10.7 0.2 convert_reduce_fusion
  10.9 0.6 pad_add_fusion.order_ref
  11.5 0.9 convolution_convert_fusion.table_ref
  12.4 104.7 %dispatch.1 = (bf16[8,16,2,8,1152]{4,3,2,1,0:T(8,128)(2,1)}, s32[16,8,8,128]{3,2,1,0:T(8,128)}) custom-call(s32[2,64]{1,0:T(2,128)} %pad_add_fusion.order_ref, s32[16,1024]{1,0:T(8,128)} %convolution_convert_fusion.table_ref, bf16[64,8,1152]{2,1,0:T(8,128)(2,1)} %emb_ref.1), custom_call_target="tpu_custom_call" | custom-call | tf_op jit(solution)/shard_map/dispatch/pallas_call | solution.py:241
  117.0 1.3 fusion.7
  118.3 1.2 add_bitcast_fusion
  119.6 0.8 copy.37
  120.4 0.2 gt.51
  120.6 0.8 copy.38
  121.4 0.2 sub.54
  121.6 0.7 convert_reduce_fusion.3
  122.3 7.5 %multiply_reduce_fusion.1 = (f32[2048]{0:T(1024)S(1)}, f32[2048,768]{1,0:T(8,128)S(1)}) fusion(f32[768]{0:T(1024)S(1)} %get-tuple-element.29, f32[768]{0:T(1024)S(1)} %get-tuple-element.30, bf16[2048,1152]{1,0:T(8,128)(2,1)} %bitcast.57, bf16[1,1152,768]{2,1,0:T(8,128)(2,1)} %param.13), kind=kOutput, calls=%fused_computation.2 | convolution fusion | flops 3634886656 | bytes 12793856 | tf_op jit(solution)/shard_map/dot_general | solution.py:296
  129.9 0.0 copy-start
  129.9 2.6 %copy-done = f32[2048,768]{1,0:T(8,128)} copy-done((f32[2048,768]{1,0:T(8,128)}, f32[2048,768]{1,0:T(8,128)S(1)}, u32[]{:S(2)}) %copy-start) | copy-done | bytes 6291480
  132.6 0.0 copy-start.1
  132.6 0.0 copy-start.2
  132.6 9.2 %fusion.1 = f32[1152,768]{1,0:T(8,128)} fusion(bf16[2048,1152]{1,0:T(8,128)(2,1)} %bitcast.58, f32[2048,768]{1,0:T(8,128)S(1)} %get-tuple-element.26, f32[2048]{0:T(1024)S(1)} %subtract_select_fusion, f32[768]{0:T(1024)S(1)} %get-tuple-element.29, f32[768]{0:T(1024)S(1)} %get-tuple-element.30), kind=kOutput, calls=%fused_computation.5 | convolution fusion | flops 3641180160 | bytes 14563328 | tf_op jit(solution)/shard_map/dot_general | solution.py:308
  141.8 0.0 all-reduce.2.cloned.1.call-update
  141.8 0.2 all-gather.2.cloned.1.call-start
  142.0 35.4 %all-reduce.2.cloned.1.call-done = f32[1152,768]{1,0:T(8,128)} async-done(((f32[1152,768]{1,0:T(8,128)}), f32[1152,768]{1,0:T(8,128)}) %all-reduce.2.cloned.1.call-update) | async-done | bytes 3538960 | tf_op jit(solution)/shard_map/psum | solution.py:311
  177.4 0.0 copy-done.1
  177.4 0.0 copy-done.2
  177.4 4.9 %fusion.9 = (f32[1,576,768]{2,1,0:T(8,128)}, bf16[576,768]{1,0:T(8,128)(2,1)}, f32[1,576,768]{2,1,0:T(8,128)}) fusion(f32[1152,768]{1,0:T(8,128)} %all-reduce.2.cloned.1.call-done, s32[]{:T(128)S(6)} %select_n.65, f32[1,576,768]{2,1,0:T(8,128)S(1)} %copy-done.1, f32[1,576,768]{2,1,0:T(8,128)S(1)} %copy-done.2, bf16[1,1152,768]{2,1,0:T(8,128)(2,1)} %param.13), kind=kLoop, calls=%fused_computation.20 | loop fusion | flops 5750784 | bytes 10616836 | tf_op jit(solution)/shard_map/broadcast_in_dim | solution.py:330
  182.4 0.0 copy-start.3
  182.4 0.0 copy-start.4
  182.4 0.0 copy-start.5
  182.4 0.0 copy-start.6
  182.4 0.0 all-gather.2.cloned.1.call-update
  182.4 5.2 %fusion.29 = (f32[768]{0:T(1024)S(1)}, f32[768]{0:T(1024)S(1)}) fusion(f32[2048,768]{1,0:T(8,128)} %copy-done, f32[768]{0:T(1024)S(1)} %get-tuple-element.30, f32[768]{0:T(1024)S(1)} %get-tuple-element.29, f32[2048]{0:T(1024)S(1)} %subtract_select_fusion), kind=kLoop, calls=%fused_computation.79 | loop fusion | flops 22018560 | bytes 6311936 | tf_op jit(solution)/shard_map/reduce_sum | solution.py:305
  187.7 2.5 %psum.15 = f32[2,768]{1,0:T(2,128)S(1)} all-reduce(f32[2,768]{1,0:T(2,128)S(1)} %pad_maximum_fusion), channel_id=1, replica_groups=mesh['dp'=32,'head'=4,'rep'=2] {'rep'}, use_global_device_ids=true, to_apply=%region_11.12 | all-reduce | flops 1536 | bytes 12288 | tf_op jit(solution)/shard_map/psum | solution.py:311
  190.2 0.0 copy-done.3
  190.2 0.0 copy-done.4
  190.2 0.0 copy-done.5
  190.2 0.0 copy-done.6
  190.2 0.6 fusion.28
  190.9 8.4 %all-gather.2.cloned.1.call-done = bf16[1152,768]{1,0:T(8,128)(2,1)} async-done(((bf16[576,768]{1,0:T(8,128)(2,1)}), bf16[1152,768]{1,0:T(8,128)(2,1)}) %all-gather.2.cloned.1.call-update) | async-done | bytes 1769488 | tf_op jit(solution)/shard_map/all_gather | solution.py:319
  199.3 2.8 %copy.41 = bf16[1,1152,768]{2,1,0:T(8,128)(2,1)} copy(bf16[1,1152,768]{2,1,0:T(8,128)(2,1)} %bitcast.53) | data formatting | bytes 3538944
  (8 shorter events, 0.1 us)
Async XLA Ops:
  7.2 170.2 %all-reduce.2.cloned.1.call-start = ((), (), s32[]{:S(2)}) async-start(), calls=%async_computation | async-start | bytes 7077888 | tf_op jit(solution)/shard_map/psum | solution.py:311
  129.9 2.7 %copy-start = (f32[2048,768]{1,0:T(8,128)}, f32[2048,768]{1,0:T(8,128)S(1)}, u32[]{:S(2)}) copy-start(f32[2048,768]{1,0:T(8,128)S(1)} %get-tuple-element.26) | copy-start | bytes 18874372
  132.6 44.9 %copy-start.1 = (f32[1,576,768]{2,1,0:T(8,128)S(1)}, f32[1,576,768]{2,1,0:T(8,128)}, u32[]{:S(2)}) copy-start(f32[1,576,768]{2,1,0:T(8,128)} %param.17) | copy-start | bytes 5308420
  132.6 44.9 %copy-start.2 = (f32[1,576,768]{2,1,0:T(8,128)S(1)}, f32[1,576,768]{2,1,0:T(8,128)}, u32[]{:S(2)}) copy-start(f32[1,576,768]{2,1,0:T(8,128)} %param.16) | copy-start | bytes 5308420
  141.8 57.5 %all-gather.2.cloned.1.call-start = ((), (), s32[]{:S(2)}) async-start(), calls=%async_computation.1 | async-start | bytes 2654208 | tf_op jit(solution)/shard_map/all_gather | solution.py:319
  182.4 7.8 %copy-start.3 = (bf16[1,768]{1,0:T(2,128)(2,1)S(1)}, bf16[1,768]{1,0:T(2,128)(2,1)}, u32[]{:S(2)}) copy-start(bf16[1,768]{1,0:T(2,128)(2,1)} %param.15) | copy-start | bytes 4612
  182.4 7.8 %copy-start.4 = (bf16[1,768]{1,0:T(2,128)(2,1)S(1)}, bf16[1,768]{1,0:T(2,128)(2,1)}, u32[]{:S(2)}) copy-start(bf16[1,768]{1,0:T(2,128)(2,1)} %param.14) | copy-start | bytes 4612
  182.4 7.9 %copy-start.5 = (f32[1,2,768]{2,1,0:T(2,128)S(1)}, f32[1,2,768]{2,1,0:T(2,128)}, u32[]{:S(2)}) copy-start(f32[1,2,768]{2,1,0:T(2,128)} %param.19) | copy-start | bytes 18436
  182.4 7.9 %copy-start.6 = (f32[1,2,768]{2,1,0:T(2,128)S(1)}, f32[1,2,768]{2,1,0:T(2,128)}, u32[]{:S(2)}) copy-start(f32[1,2,768]{2,1,0:T(2,128)} %param.18) | copy-start | bytes 18436
Sparse Core Ops, SparseCore 0:
  141.9 35.4 all-reduce.1
  182.5 16.7 all-gather.1

commit v2 on v1

v2 whole, which is shorter than its diff:
```python
import jax
import jax.numpy as jnp
from jax import lax
from jax.experimental import pallas as pl
from jax.experimental.pallas import tpu as pltpu
from jax.sharding import PartitionSpec as P

beta_one = 0.9
beta_two = 0.999
learn_rate = 0.001
epsilon = 1e-08

MESH = pl.DeviceIdType.MESH
NZ = 8
STEP_OF = (0, 1, 3, 5, 7, 6, 4, 2)
CUTS = ((0, 16), (16, 48), (48, 64))
CUTS_AT = {1: 3, 2: 3, 3: 2, 4: 1}
HOP_SIZE = (64, 64, 48, 16)


def plan(coverage, labels, z):
    blocks, top = coverage.shape
    rows = labels.shape[2]
    head = coverage
    plane = (head // 4) % NZ
    spot = (head // 32) * 4 + head % 4
    ahead = (plane - z + NZ) % NZ
    up = ((ahead >= 1) & (ahead <= 3)) | ((ahead == 4) & (spot < 8))
    far_up = jnp.max(jnp.where(up, ahead, 0), axis=1)
    far_down = jnp.max(jnp.where(up | (ahead == 0), 0, NZ - ahead), axis=1)
    number = jnp.arange(blocks, dtype=jnp.int32)

    def place(far):
        first = (far[None, :] > far[:, None]) | (
            (far[None, :] == far[:, None]) & (number[None, :] < number[:, None])
        )
        return jnp.sum(first.astype(jnp.int32), axis=1)

    pos_up, pos_down = place(far_up), place(far_down)
    order = jnp.stack(
        [
            jnp.sum(jnp.where(pos[None, :] == number[:, None], number[None, :], 0), axis=1)
            for pos in (pos_up, pos_down)
        ]
    )
    pos = jnp.where(ahead == 0, number[:, None], jnp.where(up, pos_up[:, None], pos_down[:, None]))
    entries = blocks * top
    flat = head.reshape(entries)
    nth = jnp.arange(entries, dtype=jnp.int32)
    rank = jnp.sum(
        ((flat[None, :] == flat[:, None]) & (nth[None, :] < nth[:, None])).astype(jnp.int32), axis=1
    )
    lane = (plane * 128 + spot).reshape(entries) + 16 * rank
    picker = (lane[:, None] == jnp.arange(NZ * 128, dtype=jnp.int32)[None, :]).astype(jnp.bfloat16)
    facts = jnp.concatenate(
        [
            (labels.reshape(entries, rows) + 1).astype(jnp.bfloat16),
            jnp.broadcast_to(pos.reshape(entries, 1), (entries, 8)).astype(jnp.bfloat16),
        ],
        axis=1,
    )
    table = lax.dot_general(
        facts, picker, (((0,), (0,)), ((), ())), preferred_element_type=jnp.float32
    ).astype(jnp.int32)
    return order, table


def step_kernel(
    order_ref, table_ref, emb_ref, bias_ref, out_w_ref, first_vec_ref, second_vec_ref,
    w_hbm, first_hbm, second_hbm,
    new_vec_ref, new_first_vec_ref, new_second_vec_ref, new_w_hbm, new_first_hbm, new_second_hbm,
    send_up, send_down, up_1, up_2, up_3, up_4, down_1, down_2, down_3, down_4,
    picked, got, facts, marks, w_ref, first_ref, second_ref, new_first, new_second, new_w,
    pre_ref, low_ref, turned, total, other, vec_total, vec_other, mark_col, places,
    ring_send, ring_recv, fact_send, fact_recv, place_sem, own_sem,
    mark_send, mark_recv, plane_send, plane_recv, load_sem, swap_send, swap_recv, out_sem,
):
    dp, x, core = lax.axis_index("dp"), lax.axis_index("head"), lax.axis_index("rep")
    y, z = dp // NZ, lax.rem(dp, NZ)
    me = y * 4 + x
    partner = (dp, x, 1 - core)
    feature, hid = w_ref.shape
    half = feature // 2
    piece_rows = half // 2
    f32 = jnp.float32

    def at_plane(z_to):
        return (y * NZ + z_to, x, core)

    def in_plane(j):
        p = lax.rem(me + j, 16)
        return p, ((p // 4) * NZ + z, lax.rem(p, 4), core)

    barrier = pltpu.get_barrier_semaphore()
    for d in range(1, NZ):
        pl.semaphore_signal(
            barrier, inc=1, device_id=at_plane(lax.rem(z + d, NZ)), device_id_type=MESH
        )

    def greet(j, _):
        _, device = in_plane(j)
        pl.semaphore_signal(barrier, inc=1, device_id=device, device_id_type=MESH)
        return 0

    lax.fori_loop(1, 16, greet, 0)
    pl.semaphore_signal(barrier, inc=1, device_id=partner, device_id_type=MESH)

    def arrange(i, _):
        send_up[i] = emb_ref[order_ref[0, i]]
        send_down[i] = emb_ref[order_ref[1, i]]
        return 0

    lax.fori_loop(0, 64, arrange, 0)
    own_facts = pltpu.make_async_copy(
        table_ref.at[:, pl.ds(pl.multiple_of(z * 128, 128), 128)], facts.at[0], own_sem
    )
    own_facts.start()
    own_facts.wait()
    pl.semaphore_wait(barrier, 23)

    rings = (
        (send_up, up_1, up_2, up_3, up_4),
        (send_down, down_1, down_2, down_3, down_4),
    )
    targets = (at_plane(lax.rem(z + 1, NZ)), at_plane(lax.rem(z + NZ - 1, NZ)))
    ring_copies = {}

    def hop(way, number, piece):
        low, high = CUTS[piece]
        copy = pltpu.make_async_remote_copy(
            src_ref=rings[way][number - 1].at[pl.ds(low, high - low)],
            dst_ref=rings[way][number].at[pl.ds(low, high - low)],
            send_sem=ring_send.at[way, number - 1, piece],
            recv_sem=ring_recv.at[way, number - 1, piece],
            device_id=targets[way],
            device_id_type=MESH,
        )
        copy.start()
        ring_copies[way, number, piece] = copy

    fact_copies = []
    for d in range(1, NZ):
        z_to = lax.rem(z + d, NZ)
        copy = pltpu.make_async_remote_copy(
            src_ref=table_ref.at[:, pl.ds(pl.multiple_of(z_to * 128, 128), 128)],
            dst_ref=facts.at[STEP_OF[d]],
            send_sem=fact_send.at[d],
            recv_sem=fact_recv.at[STEP_OF[d]],
            device_id=at_plane(z_to),
            device_id_type=MESH,
        )
        copy.start()
        fact_copies.append(copy)

    for piece in range(3):
        for way in range(2):
            hop(way, 1, piece)

    loads = [
        pltpu.make_async_copy(src, dst, load_sem.at[i])
        for i, (src, dst) in enumerate(
            ((w_hbm, w_ref), (first_hbm, first_ref), (second_hbm, second_ref))
        )
    ]
    for load in loads:
        load.start()

    def load_places(step):
        copy = pltpu.make_async_copy(
            facts.at[step, pl.ds(8, 8)], places.at[step], place_sem.at[step]
        )
        copy.start()
        copy.wait()

    def pick(step, way, source):
        low, high = (0, 16) if way is None else ((0, 8), (8, 16))[way]

        def one(p, _):
            picked[step, 0, p] = source[places[step, 0, p]]
            picked[step, 1, p] = source[places[step, 0, 16 + p]]
            return 0

        lax.fori_loop(low, high, one, 0)

    def spread(step):
        own = pltpu.make_async_copy(picked.at[step, :, me], got.at[step, :, me], own_sem)
        own.start()

        def send(j, _):
            p, device = in_plane(j)
            pltpu.make_async_remote_copy(
                src_ref=picked.at[step, :, p],
                dst_ref=got.at[step, :, me],
                send_sem=plane_send.at[step],
                recv_sem=plane_recv.at[step],
                device_id=device,
                device_id_type=MESH,
            ).start()
            return 0

        lax.fori_loop(1, 16, send, 0)
        own.wait()

    def received(step):
        whole = got.at[step, :, pl.ds(0, 15)]
        pltpu.make_async_copy(whole, whole, plane_recv.at[step]).wait()

    def forward(step):
        rows = got[step].reshape(256, feature)
        pre_ref[...] = jnp.dot(rows, w_ref[...], preferred_element_type=f32) + bias_ref[...].astype(f32)
        turned[...] = rows.T
        mine = marks[:, step].astype(f32).reshape(128, 128)
        lanes = lax.broadcasted_iota(jnp.int32, (128, 128), 1)
        for k in range(2):
            picked_marks = jnp.where(lanes == me + 16 * k, mine, 0.0)
            mark_col[pl.ds(128 * k, 128)] = jnp.sum(picked_marks, axis=1, keepdims=True)

        out_w = out_w_ref[...].astype(f32)

        def group(i, _):
            at = pl.ds(pl.multiple_of(i * 16, 16), 16)
            pre = pre_ref[at]
            mark = mark_col[at]
            sig = 1.0 / (1.0 + jnp.exp(-pre))
            hidden = pre * sig
            logits = jnp.sum(hidden * out_w, axis=1, keepdims=True)
            guess = 1.0 / (1.0 + jnp.exp(-logits))
            residual = jnp.where(mark > 0.5, guess - (mark - 1.0), 0.0)
            grad_pre = residual * out_w * sig * (1.0 + pre * (1.0 - sig))
            low_ref[at] = grad_pre.astype(jnp.bfloat16)
            vec_total[0] += grad_pre[0:8] + grad_pre[8:16]
            swing = residual * hidden
            vec_total[1] += swing[0:8] + swing[8:16]
            return 0

        lax.fori_loop(0, 16, group, 0)

    def gradient(low):
        at = pl.ds(pl.multiple_of(low, 16), piece_rows)
        total[at] += jnp.dot(turned[at], low_ref[...], preferred_element_type=f32)

    def learn(step, _):
        received(step)
        forward(step)
        lax.fori_loop(0, 4, lambda i, _: (gradient(i * piece_rows), 0)[1], 0)
        return 0

    load_places(0)
    pick(0, None, emb_ref)
    spread(0)

    total[...] = jnp.zeros_like(total)
    vec_total[...] = jnp.zeros_like(vec_total)

    for copy in fact_copies:
        copy.wait()
    for step in range(1, NZ):
        load_places(step)

    own_marks = pltpu.make_async_copy(facts.at[:, pl.ds(0, 8)], marks.at[me], own_sem)
    own_marks.start()

    def send_marks(j, _):
        _, device = in_plane(j)
        pltpu.make_async_remote_copy(
            src_ref=facts.at[:, pl.ds(0, 8)],
            dst_ref=marks.at[me],
            send_sem=mark_send,
            recv_sem=mark_recv,
            device_id=device,
            device_id_type=MESH,
        ).start()
        return 0

    lax.fori_loop(1, 16, send_marks, 0)
    own_marks.wait()
    for load in loads:
        load.wait()

    for number in range(1, 5):
        for piece in range(CUTS_AT[number]):
            for way in range(2):
                ring_copies[way, number, piece].wait_recv()
                if number < 4 and piece < CUTS_AT[number + 1]:
                    hop(way, number + 1, piece)
        if number < 4:
            for way in range(2):
                pick(2 * number - 1 + way, None, rings[way][number])
                spread(2 * number - 1 + way)
        else:
            pick(7, 0, up_4)
            pick(7, 1, down_4)
            spread(7)
        if number == 1:
            whole = marks.at[pl.ds(0, 15)]
            pltpu.make_async_copy(whole, whole, mark_recv).wait()
            lax.fori_loop(0, 1, learn, 0)
        elif number < 4:
            lax.fori_loop(2 * number - 3, 2 * number - 1, learn, 0)

    lax.fori_loop(5, 7, learn, 0)
    received(7)
    forward(7)

    ours = core * half
    theirs = half - ours

    def swap(i):
        copy = pltpu.make_async_remote_copy(
            src_ref=total.at[pl.ds(pl.multiple_of(theirs + i * piece_rows, 16), piece_rows)],
            dst_ref=other.at[pl.ds(i * piece_rows, piece_rows)],
            send_sem=swap_send.at[i],
            recv_sem=swap_recv.at[i],
            device_id=partner,
            device_id_type=MESH,
        )
        copy.start()
        return copy

    gradient(theirs)
    gradient(theirs + piece_rows)
    swaps = [swap(0)]
    vec_swap = pltpu.make_async_remote_copy(
        src_ref=vec_total,
        dst_ref=vec_other,
        send_sem=swap_send.at[2],
        recv_sem=swap_recv.at[2],
        device_id=partner,
        device_id_type=MESH,
    )
    vec_swap.start()
    gradient(ours)
    swaps.append(swap(1))
    gradient(ours + piece_rows)

    vec_swap.wait_recv()
    vec_sum = vec_total[...] + vec_other[...]
    grad_vec = jnp.sum(vec_sum, axis=1)
    new_first_vec = beta_one * first_vec_ref[...] + (1.0 - beta_one) * grad_vec
    new_second_vec = beta_two * second_vec_ref[...] + (1.0 - beta_two) * grad_vec * grad_vec
    vector = jnp.concatenate([bias_ref[...].astype(f32), out_w_ref[...].astype(f32)], axis=0)
    new_first_vec_ref[...] = new_first_vec
    new_second_vec_ref[...] = new_second_vec
    new_vec_ref[...] = (
        vector - learn_rate * new_first_vec / (jnp.sqrt(new_second_vec) + epsilon)
    ).astype(jnp.bfloat16)

    copies = []
    for i in range(2):
        swaps[i].wait_recv()

        def adam(r, _):
            here = pl.multiple_of(i * piece_rows + r * 16, 16)
            at = pl.ds(here, 16)
            there = pl.ds(pl.multiple_of(ours + here, 16), 16)
            grad = total[there] + other[at]
            first = beta_one * first_ref[at] + (1.0 - beta_one) * grad
            second = beta_two * second_ref[at] + (1.0 - beta_two) * grad * grad
            new_first[at] = first
            new_second[at] = second
            new_w[at] = (
                w_ref[there].astype(f32) - learn_rate * first / (jnp.sqrt(second) + epsilon)
            ).astype(jnp.bfloat16)
            return 0

        lax.fori_loop(0, piece_rows // 16, adam, 0)
        at = pl.ds(i * piece_rows, piece_rows)
        there = pl.ds(pl.multiple_of(ours + i * piece_rows, 16), piece_rows)
        for k, (src, dst) in enumerate(((new_first, new_first_hbm), (new_second, new_second_hbm))):
            copy = pltpu.make_async_copy(src.at[at], dst.at[at], out_sem.at[k, i])
            copy.start()
            copies.append(copy)
        copy = pltpu.make_async_remote_copy(
            src_ref=new_w.at[at],
            dst_ref=new_w_hbm.at[there],
            send_sem=swap_send.at[3 + i],
            recv_sem=swap_recv.at[3 + i],
            device_id=partner,
            device_id_type=MESH,
        )
        copy.start()
        copies.append(copy)
        copy = pltpu.make_async_copy(new_w.at[at], new_w_hbm.at[there], out_sem.at[2, i])
        copy.start()
        copies.append(copy)

    vec_swap.wait_send()
    for copy in swaps:
        copy.wait_send()
    for copy in ring_copies.values():
        copy.wait_send()
    whole = marks.at[pl.ds(0, 15)]
    pltpu.make_async_copy(whole, whole, mark_send).wait()
    for step in range(NZ):
        whole = got.at[step, :, pl.ds(0, 15)]
        pltpu.make_async_copy(whole, whole, plane_send.at[step]).wait()
    for copy in copies:
        copy.wait()


def per_device(
    embeddings, coverage, labels, w_in, bias_in, w_out, first_w, second_w, first_vec, second_vec
):
    feature = embeddings.shape[2]
    hid = w_in.shape[2]
    half = feature // 2
    z = lax.rem(lax.axis_index("dp"), NZ)
    order, table = plan(coverage, labels, z)
    bf16, i32, f32 = jnp.bfloat16, jnp.int32, jnp.float32
    dma, vmem = pltpu.SemaphoreType.DMA, pltpu.VMEM
    smem_in = pl.BlockSpec(memory_space=pltpu.SMEM)
    vmem_in = pl.BlockSpec(memory_space=vmem)
    any_in = pl.BlockSpec(memory_space=pl.ANY)
    new_vec, new_first_vec, new_second_vec, new_w, new_first, new_second = pl.pallas_call(
        step_kernel,
        out_shape=(
            jax.ShapeDtypeStruct((2, hid), bf16),
            jax.ShapeDtypeStruct((2, hid), f32),
            jax.ShapeDtypeStruct((2, hid), f32),
            jax.ShapeDtypeStruct((feature, hid), bf16),
            jax.ShapeDtypeStruct((half, hid), f32),
            jax.ShapeDtypeStruct((half, hid), f32),
        ),
        in_specs=[smem_in, *[vmem_in] * 6, *[any_in] * 3],
        out_specs=(*[vmem_in] * 3, *[any_in] * 3),
        scratch_shapes=[
            vmem((64, 8, feature), bf16),
            vmem((64, 8, feature), bf16),
            *[vmem((size, 8, feature), bf16) for size in HOP_SIZE * 2],
            vmem((NZ, 2, 16, 8, feature), bf16),
            vmem((NZ, 2, 16, 8, feature), bf16),
            vmem((NZ, 16, 128), i32),
            vmem((16, NZ, 8, 128), i32),
            vmem((feature, hid), bf16),
            vmem((half, hid), f32),
            vmem((half, hid), f32),
            vmem((half, hid), f32),
            vmem((half, hid), f32),
            vmem((half, hid), bf16),
            vmem((256, hid), f32),
            vmem((256, hid), bf16),
            vmem((feature, 256), bf16),
            vmem((feature, hid), f32),
            vmem((half, hid), f32),
            vmem((2, 8, hid), f32),
            vmem((2, 8, hid), f32),
            vmem((256, 1), f32),
            pltpu.SMEM((NZ, 8, 128), i32),
            dma((2, 4, 3)),
            dma((2, 4, 3)),
            dma((NZ,)),
            dma((NZ,)),
            dma((NZ,)),
            dma,
            dma,
            dma,
            dma((NZ,)),
            dma((NZ,)),
            dma((3,)),
            dma((5,)),
            dma((5,)),
            dma((3, 2)),
        ],
        compiler_params=pltpu.CompilerParams(
            collective_id=0, has_side_effects=True, vmem_limit_bytes=60 << 20
        ),
        name="adam_step",
    )(
        order, table, embeddings, bias_in, w_out, first_vec[0], second_vec[0],
        w_in[0], first_w[0], second_w[0],
    )
    return (
        new_w[None],
        new_vec[None],
        new_first[None],
        new_second[None],
        new_first_vec[None],
        new_second_vec[None],
    )


def solution(mesh):
    owners = ("dp", "head")
    moments = P(owners, "rep", None)
    vectors = P(owners, None, None)
    everyone = ("dp", "head", "rep")
    placed = (
        P(everyone, None, None),
        P(everyone, None),
        P(everyone, None, None),
        vectors,
        P(owners, None),
        P(owners, None),
        moments,
        moments,
        vectors,
        vectors,
    )
    return jax.shard_map(
        per_device,
        mesh=mesh,
        in_specs=placed,
        out_specs=(vectors, vectors, moments, moments, vectors, vectors),
        check_vma=False,
    )
```

time: 211 us -> 137 us (0.65)
  the two profiles are of different devices: /device:TPU:25 before, /device:TPU:1 now
where the time goes in v2:
time: 137 us; the launch traced here: 136 us
  Pallas kernels  122 us (89%)
  local copies, waits for them, and re-layouts  9.62 us (7%)
  other arithmetic  2.61 us (2%)
    pallas_call x1, Pallas kernels, per_device(): pl.pallas_call(step_kernel, out_shape=(jax.ShapeDtypeStruct((2, hid), bf1...  122 us
    unnamed x17, local copies, waits for them, and re-layouts  8.8 us

profile of v2, /device:TPU:1, one launch (start us, length us, event | category | flops | bytes accessed | tf_op | source)
XLA Modules:
  0.0 136.3 jit_solution(4904537770196047211)
XLA Ops:
  0.6 0.7 multiply_add_fusion
  1.4 0.2 convert_reduce_fusion.1
  1.6 0.1 select_reduce_fusion.1
  1.7 0.1 select_reduce_fusion
  1.8 0.6 pad_add_fusion.order_ref
  2.4 0.7 add_convert_fusion
  3.1 0.1 copy.29
  3.2 0.1 convert_element_type.31
  3.4 0.1 copy.28
  3.5 0.1 copy.30
  3.5 0.1 copy.31
  3.6 0.2 reshape.40
  3.8 0.8 copy.32
  4.6 0.1 eq.42
  4.7 0.2 convert_reduce_fusion
  4.9 0.9 convolution_convert_fusion.table_ref
  5.8 122.5 %adam_step.1 = (bf16[2,768]{1,0:T(2,128)(2,1)}, f32[2,768]{1,0:T(2,128)}, f32[2,768]{1,0:T(2,128)}, bf16[1152,768]{1,0:T(8,128)(2,1)}, f32[576,768]{1,0:T(8,128)}, /*index=5*/f32[576,768]{1,0:T(8,128)}) custom-call(s32[2,64]{1,0:T(2,128)} %pad_add_fusion.order_ref, s32[16,1024]{1,0:T(8,128)} %convolution_convert_fusion.table_ref, ...), custom_call_target="tpu_custom_call" | custom-call | tf_op jit(solution)/shard_map/adam_step/pallas_call | solution.py:414
  128.3 0.0 copy-start.4
  128.3 0.0 copy-start.1
  128.3 2.9 %copy.39 = bf16[1,1152,768]{2,1,0:T(8,128)(2,1)} copy(bf16[1,1152,768]{2,1,0:T(8,128)(2,1)} %bitcast.19) | data formatting | bytes 3538944
  131.2 0.0 copy-done.4
  131.2 0.6 copy.40
  131.8 0.0 copy-done.1
  131.8 0.0 copy-start
  131.8 1.2 copy.41
  133.0 0.9 copy-done
  133.9 0.0 copy-start.3
  133.9 0.0 copy-start.2
  133.9 1.2 copy.42
  135.2 0.0 copy-done.3
  135.2 0.6 copy.43
  135.7 0.0 copy-done.2
  135.8 0.6 copy.44
  (4 shorter events, 0.1 us)
Async XLA Ops:
  128.3 2.9 %copy-start.4 = (bf16[2,768]{1,0:T(2,128)(2,1)S(1)}, bf16[2,768]{1,0:T(2,128)(2,1)}, u32[]{:S(2)}) copy-start(bf16[2,768]{1,0:T(2,128)(2,1)} %get-tuple-element.13) | copy-start | bytes 9220
  128.3 3.5 %copy-start.1 = (f32[576,768]{1,0:T(8,128)S(1)}, f32[576,768]{1,0:T(8,128)}, u32[]{:S(2)}) copy-start(f32[576,768]{1,0:T(8,128)} %get-tuple-element.14) | copy-start | bytes 5308420
  131.8 2.1 %copy-start = (f32[576,768]{1,0:T(8,128)S(1)}, f32[576,768]{1,0:T(8,128)}, u32[]{:S(2)}) copy-start(f32[576,768]{1,0:T(8,128)} %get-tuple-element.15) | copy-start | bytes 5308420
  133.9 1.2 copy-start.3
  133.9 1.8 %copy-start.2 = (f32[2,768]{1,0:T(2,128)S(1)}, f32[2,768]{1,0:T(2,128)}, u32[]{:S(2)}) copy-start(f32[2,768]{1,0:T(2,128)} %get-tuple-element.17) | copy-start | bytes 18436

commit v3 on v2

v3 whole, which is shorter than its diff:
```python
import jax
import jax.numpy as jnp
from jax import lax
from jax.experimental import pallas as pl
from jax.experimental.pallas import tpu as pltpu
from jax.sharding import PartitionSpec as P

beta_one = 0.9
beta_two = 0.999
learn_rate = 0.001
epsilon = 1e-08

MESH = pl.DeviceIdType.MESH
NZ = 8
STEP_OF = (0, 1, 3, 5, 7, 6, 4, 2)
PIECES = {
    1: ((0, 24), (24, 48), (48, 64)),
    2: ((0, 24), (24, 48), (48, 64)),
    3: ((0, 24), (24, 32), (32, 40), (40, 48)),
    4: ((0, 16),),
}


def plan_kernel(cover_ref, labels_ref, order_ref, table_ref):
    z = lax.rem(lax.axis_index("dp"), NZ)
    f32, i32, bf16 = jnp.float32, jnp.int32, jnp.bfloat16
    blocks = 64
    square = (blocks, blocks)
    down_axis = lax.broadcasted_iota(i32, square, 0)
    along = lax.broadcasted_iota(i32, square, 1)
    number = lax.broadcasted_iota(i32, (1, blocks), 1)

    def upright(row):
        spread = jnp.where(down_axis == along, jnp.broadcast_to(row, square), 0)
        return jnp.sum(spread.astype(f32), axis=1, keepdims=True).astype(i32)

    def count(flags):
        return jnp.sum(jnp.where(flags, 1.0, 0.0), axis=0, keepdims=True).astype(i32)

    heads = [cover_ref[t : t + 1] for t in range(2)]
    ahead, spot, up, far_up, far_down = [], [], [], None, None
    for head in heads:
        plane = (head >> 2) & 7
        x, y = head & 3, head >> 5
        kind = (x + y) & 3
        gap = (plane - z + NZ) & 7
        is_up = ((gap >= 1) & (gap <= 3)) | ((gap == 4) & (kind < 2))
        is_down = (gap >= 5) | ((gap == 4) & (kind >= 2))
        rank_up = jnp.where(gap == 4, 9, jnp.where(gap == 3, 8 - kind, 0))
        rank_down = jnp.where(gap == 4, 9, jnp.where(gap == 5, 8 - kind, 0))
        rank_up = jnp.where(is_up, rank_up, 0)
        rank_down = jnp.where(is_down, rank_down, 0)
        far_up = rank_up if far_up is None else jnp.maximum(far_up, rank_up)
        far_down = rank_down if far_down is None else jnp.maximum(far_down, rank_down)
        ahead.append(gap)
        spot.append(4 * kind + x)
        up.append(is_up)

    places, orders = [], []
    for far in (far_up, far_down):
        tall = upright(far)
        pos = count((tall > far) | ((tall == far) & (down_axis < along)))
        places.append(pos)
        order = jnp.sum(
            jnp.where(upright(pos) == along, down_axis, 0).astype(f32), axis=0, keepdims=True
        )
        orders.append(order.astype(i32))
    order_ref[0:1] = orders[0]
    order_ref[1:2] = orders[1]

    tall_heads = [upright(head) for head in heads]
    earlier = down_axis < along
    ranks = [
        count((tall_heads[0] == heads[0]) & earlier),
        count(tall_heads[0] == heads[1]) + count((tall_heads[1] == heads[1]) & earlier),
    ]
    row = lax.broadcasted_iota(i32, (8, blocks), 0)
    lanes = lax.broadcasted_iota(i32, (blocks, NZ * 128), 1)
    table = None
    for t in range(2):
        plane, gap = (heads[t] >> 2) & 7, ahead[t]
        step = jnp.where(gap < 4, jnp.maximum(2 * gap - 1, 0), jnp.where(gap == 4, 7, 2 * (NZ - gap)))
        lane = plane * 128 + step * 16 + spot[t]
        picker = jnp.where(upright(lane) == lanes, 1.0, 0.0).astype(bf16)
        pos = jnp.where(gap == 0, number, jnp.where(up[t], places[0], places[1]))
        mark = labels_ref[t] + 1
        rank = jnp.broadcast_to(ranks[t], (8, blocks))
        tall_pos = jnp.broadcast_to(pos, (8, blocks))
        facts = jnp.concatenate(
            [
                jnp.where(rank == 0, mark, 0).astype(f32),
                jnp.where(rank == 1, mark, 0).astype(f32),
                jnp.where(rank == row, tall_pos, 0).astype(f32),
            ],
            axis=0,
        ).astype(bf16)
        part = jnp.dot(facts, picker, preferred_element_type=f32)
        table = part if table is None else table + part
    table_ref[...] = table.astype(i32)


def step_kernel(
    order_ref, table_ref, emb_ref, bias_ref, out_w_ref, first_vec_ref, second_vec_ref,
    w_hbm, first_hbm, second_hbm,
    new_vec_ref, new_first_vec_ref, new_second_vec_ref, new_w_hbm, new_first_hbm, new_second_hbm,
    send_up, send_down,
    up_1, up_2, up_3a, up_3b, up_3c, up_3d, up_4,
    down_1, down_2, down_3a, down_3b, down_3c, down_3d, down_4,
    up_3, down_3, picked, got, facts, own_marks, marks, w_ref, first_ref, second_ref, new_first, new_second, new_w,
    pre_ref, low_ref, turned, total, other, vec_total, vec_other, mark_col, places,
    ring_send, ring_recv, fact_send, fact_recv, place_sem, own_sem,
    mark_send, mark_recv, plane_send, plane_recv, load_sem, swap_send, swap_recv, out_sem,
):
    dp, x, core = lax.axis_index("dp"), lax.axis_index("head"), lax.axis_index("rep")
    y, z = dp // NZ, lax.rem(dp, NZ)
    me = 4 * lax.rem(x + y, 4) + x
    partner = (dp, x, 1 - core)
    feature, hid = w_ref.shape
    half = feature // 2
    piece_rows = half // 2
    f32 = jnp.float32

    def at_plane(z_to):
        return (y * NZ + z_to, x, core)

    def spot_device(p):
        x_to = lax.rem(p, 4)
        return (lax.rem(p // 4 - x_to + 4, 4) * NZ + z, x_to, core)

    barrier = pltpu.get_barrier_semaphore()
    for d in range(1, NZ):
        pl.semaphore_signal(
            barrier, inc=1, device_id=at_plane(lax.rem(z + d, NZ)), device_id_type=MESH
        )

    def greet(j, _):
        device = spot_device(lax.rem(me + j, 16))
        pl.semaphore_signal(barrier, inc=1, device_id=device, device_id_type=MESH)
        return 0

    lax.fori_loop(1, 16, greet, 0)
    pl.semaphore_signal(barrier, inc=1, device_id=partner, device_id_type=MESH)

    def arrange(i, _):
        send_up[i] = emb_ref[order_ref[0, i]]
        send_down[i] = emb_ref[order_ref[1, i]]
        return 0

    lax.fori_loop(0, 64, arrange, 0, unroll=4)
    own_facts = pltpu.make_async_copy(
        table_ref.at[:, pl.ds(pl.multiple_of(z * 128, 128), 128)], facts.at[0], load_sem.at[3]
    )
    own_facts.start()
    pl.semaphore_wait(barrier, 23)

    def whole(ref, number):
        return [ref.at[pl.ds(low, high - low)] for low, high in PIECES[number]]

    thirds = ((up_3a, up_3b, up_3c, up_3d), (down_3a, down_3b, down_3c, down_3d))
    arrivals = (
        {1: whole(up_1, 1), 2: whole(up_2, 2), 3: thirds[0], 4: (up_4,)},
        {1: whole(down_1, 1), 2: whole(down_2, 2), 3: thirds[1], 4: (down_4,)},
    )
    targets = (at_plane(lax.rem(z + 1, NZ)), at_plane(lax.rem(z + NZ - 1, NZ)))
    sources = ({1: send_up, 2: up_1, 3: up_2}, {1: send_down, 2: down_1, 3: down_2})
    ring_copies = {}

    def hop(way, number, piece):
        low, high = PIECES[number][piece]
        src = thirds[way][0] if number == 4 else sources[way][number]
        copy = pltpu.make_async_remote_copy(
            src_ref=src.at[pl.ds(low, high - low)],
            dst_ref=arrivals[way][number][piece],
            send_sem=ring_send.at[way, number - 1, piece],
            recv_sem=ring_recv.at[way, number - 1, piece],
            device_id=targets[way],
            device_id_type=MESH,
        )
        copy.start()
        ring_copies[way, number, piece] = copy

    fact_copies = []
    for d in range(1, NZ):
        z_to = lax.rem(z + d, NZ)
        copy = pltpu.make_async_remote_copy(
            src_ref=table_ref.at[:, pl.ds(pl.multiple_of(z_to * 128, 128), 128)],
            dst_ref=facts.at[STEP_OF[d]],
            send_sem=fact_send.at[d],
            recv_sem=fact_recv.at[STEP_OF[d]],
            device_id=at_plane(z_to),
            device_id_type=MESH,
        )
        copy.start()
        fact_copies.append(copy)

    for piece in range(3):
        for way in range(2):
            hop(way, 1, piece)

    loads = [
        pltpu.make_async_copy(src, dst, load_sem.at[i])
        for i, (src, dst) in enumerate(
            ((w_hbm, w_ref), (first_hbm, first_ref), (second_hbm, second_ref))
        )
    ]
    for load in loads:
        load.start()

    def pick(step, source, first, last):
        def one(p, _):
            for k in range(2):
                picked[step, k, p] = source[places[step, k, step * 16 + p]]
            return 0

        lax.fori_loop(4 * first, 4 * last, one, 0, unroll=4)

    def spread(step, first, last):
        def send(j, _):
            p = (j // 4) * 4 + lax.rem(x + j, 4)

            @pl.when(p != me)
            def _():
                pltpu.make_async_remote_copy(
                    src_ref=picked.at[step, :, p],
                    dst_ref=got.at[step, :, me],
                    send_sem=plane_send.at[step],
                    recv_sem=plane_recv.at[step],
                    device_id=spot_device(p),
                    device_id_type=MESH,
                ).start()

            @pl.when(p == me)
            def _():
                pltpu.make_async_copy(
                    picked.at[step, :, me], got.at[step, :, me], own_sem.at[step]
                ).start()

            return 0

        lax.fori_loop(4 * first, 4 * last, send, 0)

    def received(step):
        most = got.at[step, :, pl.ds(0, 15)]
        pltpu.make_async_copy(most, most, plane_recv.at[step]).wait()
        pltpu.make_async_copy(picked.at[step, :, me], got.at[step, :, me], own_sem.at[step]).wait()

    def forward(step):
        rows = got[step].reshape(256, feature)
        pre_ref[...] = jnp.dot(rows, w_ref[...], preferred_element_type=f32) + bias_ref[...].astype(f32)
        turned[...] = rows.T
        lanes = lax.broadcasted_iota(jnp.int32, (128, 128), 1)
        for k in range(2):
            every = marks[:, 8 * k : 8 * k + 8].astype(f32).reshape(128, 128)
            picked_marks = jnp.where(lanes == me + 16 * step, every, 0.0)
            mark_col[pl.ds(128 * k, 128)] = jnp.sum(picked_marks, axis=1, keepdims=True)

        out_w = out_w_ref[...].astype(f32)

        def group(i, _):
            at = pl.ds(pl.multiple_of(i * 16, 16), 16)
            pre = pre_ref[at]
            mark = mark_col[at]
            sig = 1.0 / (1.0 + jnp.exp(-pre))
            hidden = pre * sig
            logits = jnp.sum(hidden * out_w, axis=1, keepdims=True)
            guess = 1.0 / (1.0 + jnp.exp(-logits))
            residual = jnp.where(mark > 0.5, guess - (mark - 1.0), 0.0)
            grad_pre = residual * out_w * sig * (1.0 + pre * (1.0 - sig))
            low_ref[at] = grad_pre.astype(jnp.bfloat16)
            vec_total[0] += grad_pre[0:8] + grad_pre[8:16]
            swing = residual * hidden
            vec_total[1] += swing[0:8] + swing[8:16]
            return 0

        lax.fori_loop(0, 16, group, 0, unroll=4)

    def gradient(low, rows):
        at = pl.ds(pl.multiple_of(low, 16), rows)
        total[at] += jnp.dot(turned[at], low_ref[...], preferred_element_type=f32)

    def learn(step, _):
        received(step)
        forward(step)
        for i in range(2):
            gradient(i * half, half)
        return 0

    total[...] = jnp.zeros_like(total)
    vec_total[...] = jnp.zeros_like(vec_total)

    for copy in fact_copies:
        copy.wait()
    own_facts.wait()
    place_copies = []
    for step in range(NZ):
        copy = pltpu.make_async_copy(
            facts.at[step, pl.ds(16, 8)], places.at[step], place_sem.at[step]
        )
        copy.start()
        place_copies.append(copy)
    joined = facts[0, 0:16]
    for step in range(1, NZ):
        joined = joined + facts[step, 0:16]
    own_marks[...] = joined
    for copy in place_copies:
        copy.wait()
    pick(0, emb_ref, 0, 4)
    spread(0, 0, 4)
    marks[me] = joined

    def send_marks(j, _):
        pltpu.make_async_remote_copy(
            src_ref=own_marks,
            dst_ref=marks.at[me],
            send_sem=mark_send,
            recv_sem=mark_recv,
            device_id=spot_device(lax.rem(me + j, 16)),
            device_id_type=MESH,
        ).start()
        return 0

    lax.fori_loop(1, 16, send_marks, 0)
    for load in loads:
        load.wait()

    for piece in range(3):
        for way in range(2):
            ring_copies[way, 1, piece].wait_recv()
            hop(way, 2, piece)
    pick(1, up_1, 0, 4)
    pick(2, down_1, 0, 4)
    spread(1, 0, 4)
    spread(2, 0, 4)
    most_marks = marks.at[pl.ds(0, 15)]
    pltpu.make_async_copy(most_marks, most_marks, mark_recv).wait()
    lax.fori_loop(0, 1, learn, 0)

    for piece in range(3):
        for way in range(2):
            ring_copies[way, 2, piece].wait_recv()
            if piece == 0:
                hop(way, 3, 0)
            elif piece == 1:
                for part in (1, 2, 3):
                    hop(way, 3, part)
    pick(3, up_2, 0, 4)
    pick(4, down_2, 0, 4)
    spread(3, 0, 4)
    spread(4, 0, 4)
    lax.fori_loop(1, 3, learn, 0)

    for kind in range(4):
        low, high = PIECES[3][kind]
        for way, joint in enumerate((up_3, down_3)):
            ring_copies[way, 3, kind].wait_recv()
            if kind == 0:
                hop(way, 4, 0)
            joint[pl.ds(low, high - low)] = thirds[way][kind][...]
            pick(5 + way, joint, kind, kind + 1)
        spread(5, kind, kind + 1)
        spread(6, kind, kind + 1)
    lax.fori_loop(3, 5, learn, 0)

    for way, source in enumerate((up_4, down_4)):
        ring_copies[way, 4, 0].wait_recv()
        pick(7, source, 2 * way, 2 * way + 2)
    spread(7, 0, 4)
    lax.fori_loop(5, 7, learn, 0)
    received(7)
    forward(7)

    ours = core * half
    theirs = half - ours

    def swap(i):
        copy = pltpu.make_async_remote_copy(
            src_ref=total.at[pl.ds(pl.multiple_of(theirs + i * piece_rows, 16), piece_rows)],
            dst_ref=other.at[pl.ds(i * piece_rows, piece_rows)],
            send_sem=swap_send.at[i],
            recv_sem=swap_recv.at[i],
            device_id=partner,
            device_id_type=MESH,
        )
        copy.start()
        return copy

    gradient(theirs, half)
    swaps = [swap(0), swap(1)]
    vec_swap = pltpu.make_async_remote_copy(
        src_ref=vec_total,
        dst_ref=vec_other,
        send_sem=swap_send.at[2],
        recv_sem=swap_recv.at[2],
        device_id=partner,
        device_id_type=MESH,
    )
    vec_swap.start()
    gradient(ours, half)

    vec_swap.wait_recv()
    vec_sum = vec_total[...] + vec_other[...]
    grad_vec = jnp.sum(vec_sum, axis=1)
    new_first_vec = beta_one * first_vec_ref[...] + (1.0 - beta_one) * grad_vec
    new_second_vec = beta_two * second_vec_ref[...] + (1.0 - beta_two) * grad_vec * grad_vec
    vector = jnp.concatenate([bias_ref[...].astype(f32), out_w_ref[...].astype(f32)], axis=0)
    new_first_vec_ref[...] = new_first_vec
    new_second_vec_ref[...] = new_second_vec
    new_vec_ref[...] = (
        vector - learn_rate * new_first_vec / (jnp.sqrt(new_second_vec) + epsilon)
    ).astype(jnp.bfloat16)

    copies = []
    for i in range(2):
        swaps[i].wait_recv()

        def adam(r, _):
            here = pl.multiple_of(i * piece_rows + r * 16, 16)
            at = pl.ds(here, 16)
            there = pl.ds(pl.multiple_of(ours + here, 16), 16)
            grad = total[there] + other[at]
            first = beta_one * first_ref[at] + (1.0 - beta_one) * grad
            second = beta_two * second_ref[at] + (1.0 - beta_two) * grad * grad
            new_first[at] = first
            new_second[at] = second
            new_w[at] = (
                w_ref[there].astype(f32) - learn_rate * first / (jnp.sqrt(second) + epsilon)
            ).astype(jnp.bfloat16)
            return 0

        lax.fori_loop(0, piece_rows // 16, adam, 0, unroll=3)
        at = pl.ds(i * piece_rows, piece_rows)
        there = pl.ds(pl.multiple_of(ours + i * piece_rows, 16), piece_rows)
        for k, (src, dst) in enumerate(((new_first, new_first_hbm), (new_second, new_second_hbm))):
            copy = pltpu.make_async_copy(src.at[at], dst.at[at], out_sem.at[k, i])
            copy.start()
            copies.append(copy)
        copy = pltpu.make_async_remote_copy(
            src_ref=new_w.at[at],
            dst_ref=new_w_hbm.at[there],
            send_sem=swap_send.at[3 + i],
            recv_sem=swap_recv.at[3 + i],
            device_id=partner,
            device_id_type=MESH,
        )
        copy.start()
        copies.append(copy)
        copy = pltpu.make_async_copy(new_w.at[at], new_w_hbm.at[there], out_sem.at[2, i])
        copy.start()
        copies.append(copy)

    vec_swap.wait_send()
    for copy in swaps:
        copy.wait_send()
    for copy in ring_copies.values():
        copy.wait_send()
    pltpu.make_async_copy(most_marks, most_marks, mark_send).wait()
    for step in range(NZ):
        most = got.at[step, :, pl.ds(0, 15)]
        pltpu.make_async_copy(most, most, plane_send.at[step]).wait()
    for copy in copies:
        copy.wait()


def per_device(
    embeddings, coverage, labels, w_in, bias_in, w_out, first_w, second_w, first_vec, second_vec
):
    feature = embeddings.shape[2]
    hid = w_in.shape[2]
    half = feature // 2
    bf16, i32, f32 = jnp.bfloat16, jnp.int32, jnp.float32
    dma, vmem = pltpu.SemaphoreType.DMA, pltpu.VMEM
    smem_in = pl.BlockSpec(memory_space=pltpu.SMEM)
    vmem_in = pl.BlockSpec(memory_space=vmem)
    any_in = pl.BlockSpec(memory_space=pl.ANY)
    order, table = pl.pallas_call(
        plan_kernel,
        out_shape=(
            jax.ShapeDtypeStruct((2, 64), i32),
            jax.ShapeDtypeStruct((24, NZ * 128), i32),
        ),
        in_specs=[vmem_in] * 2,
        out_specs=(vmem_in, vmem_in),
        name="plan",
    )(coverage.T, labels.transpose(1, 2, 0))
    new_vec, new_first_vec, new_second_vec, new_w, new_first, new_second = pl.pallas_call(
        step_kernel,
        out_shape=(
            jax.ShapeDtypeStruct((2, hid), bf16),
            jax.ShapeDtypeStruct((2, hid), f32),
            jax.ShapeDtypeStruct((2, hid), f32),
            jax.ShapeDtypeStruct((feature, hid), bf16),
            jax.ShapeDtypeStruct((half, hid), f32),
            jax.ShapeDtypeStruct((half, hid), f32),
        ),
        in_specs=[smem_in, *[vmem_in] * 6, *[any_in] * 3],
        out_specs=(*[vmem_in] * 3, *[any_in] * 3),
        scratch_shapes=[
            vmem((64, 8, feature), bf16),
            vmem((64, 8, feature), bf16),
            *[vmem((size, 8, feature), bf16) for size in (64, 64, 24, 8, 8, 8, 16) * 2],
            vmem((48, 8, feature), bf16),
            vmem((48, 8, feature), bf16),
            vmem((NZ, 2, 16, 8, feature), bf16),
            vmem((NZ, 2, 16, 8, feature), bf16),
            vmem((NZ, 24, 128), i32),
            vmem((16, 128), i32),
            vmem((16, 16, 128), i32),
            vmem((feature, hid), bf16),
            vmem((half, hid), f32),
            vmem((half, hid), f32),
            vmem((half, hid), f32),
            vmem((half, hid), f32),
            vmem((half, hid), bf16),
            vmem((256, hid), f32),
            vmem((256, hid), bf16),
            vmem((feature, 256), bf16),
            vmem((feature, hid), f32),
            vmem((half, hid), f32),
            vmem((2, 8, hid), f32),
            vmem((2, 8, hid), f32),
            vmem((256, 1), f32),
            pltpu.SMEM((NZ, 8, 128), i32),
            dma((2, 4, 4)),
            dma((2, 4, 4)),
            dma((NZ,)),
            dma((NZ,)),
            dma((NZ,)),
            dma((NZ,)),
            dma,
            dma,
            dma((NZ,)),
            dma((NZ,)),
            dma((4,)),
            dma((5,)),
            dma((5,)),
            dma((3, 2)),
        ],
        compiler_params=pltpu.CompilerParams(
            collective_id=0, has_side_effects=True, vmem_limit_bytes=60 << 20
        ),
        name="adam_step",
    )(
        order, table, embeddings, bias_in, w_out, first_vec[0], second_vec[0],
        w_in[0], first_w[0], second_w[0],
    )
    return (
        new_w[None],
        new_vec[None],
        new_first[None],
        new_second[None],
        new_first_vec[None],
        new_second_vec[None],
    )


def solution(mesh):
    owners = ("dp", "head")
    moments = P(owners, "rep", None)
    vectors = P(owners, None, None)
    everyone = ("dp", "head", "rep")
    placed = (
        P(everyone, None, None),
        P(everyone, None),
        P(everyone, None, None),
        vectors,
        P(owners, None),
        P(owners, None),
        moments,
        moments,
        vectors,
        vectors,
    )
    return jax.shard_map(
        per_device,
        mesh=mesh,
        in_specs=placed,
        out_specs=(vectors, vectors, moments, moments, vectors, vectors),
        check_vma=False,
    )
```

time: 137 us -> 131 us (0.956)
  the two profiles are of different devices: /device:TPU:1 before, /device:TPU:25 now
where the time goes in v3:
time: 131 us; the launch traced here: 130 us
  Pallas kernels  122 us (93%)
  local copies, waits for them, and re-layouts  8.03 us (6%)
    pallas_call x1, Pallas kernels, per_device(): pl.pallas_call(step_kernel, out_shape=(jax.ShapeDtypeStruct((2, hid), bf1...  120 us
    unnamed x16, local copies, waits for them, and re-layouts  8.03 us

profile of v3, /device:TPU:25, one launch (start us, length us, event | category | flops | bytes accessed | tf_op | source)
XLA Modules:
  0.0 130.4 jit_solution(9706666282375222541)
XLA Ops:
  0.6 1.7 %plan.1 = (s32[2,64]{1,0:T(2,128)}, s32[24,1024]{1,0:T(8,128)}) custom-call(s32[2,64]{1,0:T(2,128)} %bitcast.25, s32[2,8,64]{2,1,0:T(8,128)} %bitcast.19), custom_call_target="tpu_custom_call" | custom-call | tf_op jit(solution)/shard_map/plan/pallas_call | solution.py:475
  2.3 120.1 %adam_step.1 = (bf16[2,768]{1,0:T(2,128)(2,1)}, f32[2,768]{1,0:T(2,128)}, f32[2,768]{1,0:T(2,128)}, bf16[1152,768]{1,0:T(8,128)(2,1)}, f32[576,768]{1,0:T(8,128)}, /*index=5*/f32[576,768]{1,0:T(8,128)}) custom-call(s32[2,64]{1,0:T(2,128)} %get-tuple-element.14.order_ref, s32[24,1024]{1,0:T(8,128)} %get-tuple-element.15.table_ref, ...), custom_call_target="tpu_custom_call" | custom-call | tf_op jit(solution)/shard_map/adam_step/pallas_call | solution.py:485
  122.4 0.0 copy-start.4
  122.4 0.0 copy-start.1
  122.4 2.9 %copy.22 = bf16[1,1152,768]{2,1,0:T(8,128)(2,1)} copy(bf16[1,1152,768]{2,1,0:T(8,128)(2,1)} %bitcast.18) | data formatting | bytes 3538944
  125.3 0.0 copy-done.4
  125.3 0.6 copy.23
  125.9 0.0 copy-done.1
  125.9 0.0 copy-start
  125.9 1.2 copy.24
  127.1 0.9 copy-done
  128.0 0.0 copy-start.3
  128.0 0.0 copy-start.2
  128.0 1.2 copy.25
  129.2 0.0 copy-done.3
  129.2 0.6 copy.26
  129.8 0.0 copy-done.2
  129.8 0.6 copy.27
Async XLA Ops:
  122.4 2.9 %copy-start.4 = (bf16[2,768]{1,0:T(2,128)(2,1)S(1)}, bf16[2,768]{1,0:T(2,128)(2,1)}, u32[]{:S(2)}) copy-start(bf16[2,768]{1,0:T(2,128)(2,1)} %get-tuple-element.17) | copy-start | bytes 9220
  122.4 3.5 %copy-start.1 = (f32[576,768]{1,0:T(8,128)S(1)}, f32[576,768]{1,0:T(8,128)}, u32[]{:S(2)}) copy-start(f32[576,768]{1,0:T(8,128)} %get-tuple-element.18) | copy-start | bytes 5308420
  125.9 2.1 %copy-start = (f32[576,768]{1,0:T(8,128)S(1)}, f32[576,768]{1,0:T(8,128)}, u32[]{:S(2)}) copy-start(f32[576,768]{1,0:T(8,128)} %get-tuple-element.19) | copy-start | bytes 5308420
  128.0 1.2 copy-start.3
  128.0 1.8 %copy-start.2 = (f32[2,768]{1,0:T(2,128)S(1)}, f32[2,768]{1,0:T(2,128)}, u32[]{:S(2)}) copy-start(f32[2,768]{1,0:T(2,128)} %get-tuple-element.21) | copy-start | bytes 18436

commit v4 on v3

--- a/solution.py
+++ b/solution.py
@@ -14,14 +14,14 @@
 NZ = 8
 STEP_OF = (0, 1, 3, 5, 7, 6, 4, 2)
 PIECES = {
-    1: ((0, 24), (24, 48), (48, 64)),
-    2: ((0, 24), (24, 48), (48, 64)),
+    1: ((0, 24), (24, 48), (48, 56), (56, 64)),
+    2: ((0, 24), (24, 48), (48, 56), (56, 64)),
     3: ((0, 24), (24, 32), (32, 40), (40, 48)),
-    4: ((0, 16),),
+    4: ((0, 8), (8, 16)),
 }
 
 
-def plan_kernel(cover_ref, labels_ref, order_ref, table_ref):
+def plan_kernel(cover_ref, labels_ref, order_ref, marks_ref, spots_ref):
     z = lax.rem(lax.axis_index("dp"), NZ)
     f32, i32, bf16 = jnp.float32, jnp.int32, jnp.bfloat16
     blocks = 64
@@ -46,8 +46,11 @@
         gap = (plane - z + NZ) & 7
         is_up = ((gap >= 1) & (gap <= 3)) | ((gap == 4) & (kind < 2))
         is_down = (gap >= 5) | ((gap == 4) & (kind >= 2))
-        rank_up = jnp.where(gap == 4, 9, jnp.where(gap == 3, 8 - kind, 0))
-        rank_down = jnp.where(gap == 4, 9, jnp.where(gap == 5, 8 - kind, 0))
+        near = jnp.where(kind == 0, 4, 0)
+        rank_up = jnp.where(gap == 3, 8 - kind, jnp.where(gap == 2, near, 0))
+        rank_down = jnp.where(gap == 5, 8 - kind, jnp.where(gap == 6, near, 0))
+        rank_up = jnp.where(gap == 4, 10 - (kind & 1), rank_up)
+        rank_down = jnp.where(gap == 4, 10 - (kind & 1), rank_down)
         rank_up = jnp.where(is_up, rank_up, 0)
         rank_down = jnp.where(is_down, rank_down, 0)
         far_up = rank_up if far_up is None else jnp.maximum(far_up, rank_up)
@@ -96,20 +99,25 @@
         ).astype(bf16)
         part = jnp.dot(facts, picker, preferred_element_type=f32)
         table = part if table is None else table + part
-    table_ref[...] = table.astype(i32)
+    for plane in range(NZ):
+        part = table[:, plane * 128 : plane * 128 + 128]
+        marks_ref[plane] = part[0:16].astype(bf16)
+        spots_ref[plane] = part[16:18].astype(i32)
 
 
 def step_kernel(
-    order_ref, table_ref, emb_ref, bias_ref, out_w_ref, first_vec_ref, second_vec_ref,
+    order_ref, plan_marks, plan_spots, emb_ref, bias_ref, out_w_ref, first_vec_ref, second_vec_ref,
     w_hbm, first_hbm, second_hbm,
-    new_vec_ref, new_first_vec_ref, new_second_vec_ref, new_w_hbm, new_first_hbm, new_second_hbm,
+    new_vec_ref, new_first_vec_ref, new_second_vec_ref, new_w, new_first, new_second,
     send_up, send_down,
-    up_1, up_2, up_3a, up_3b, up_3c, up_3d, up_4,
-    down_1, down_2, down_3a, down_3b, down_3c, down_3d, down_4,
-    up_3, down_3, picked, got, facts, own_marks, marks, w_ref, first_ref, second_ref, new_first, new_second, new_w,
-    pre_ref, low_ref, turned, total, other, vec_total, vec_other, mark_col, places,
+    up_1, up_2a, up_2b, up_3a, up_3b, up_3c, up_3d, up_4a, up_4b,
+    down_1, down_2a, down_2b, down_3a, down_3b, down_3c, down_3d, down_4a, down_4b,
+    up_2, up_3, up_4, down_2, down_3, down_4,
+    picked, got, facts, spots, own_marks, marks, w_ref, first_ref, second_ref,
+    pre_ref, low_ref, low_other, turned, turned_other, total, other, vec_total, vec_other,
+    mark_col, places,
     ring_send, ring_recv, fact_send, fact_recv, place_sem, own_sem,
-    mark_send, mark_recv, plane_send, plane_recv, load_sem, swap_send, swap_recv, out_sem,
+    mark_send, mark_recv, plane_send, plane_recv, load_sem, swap_send, swap_recv,
 ):
     dp, x, core = lax.axis_index("dp"), lax.axis_index("head"), lax.axis_index("rep")
     y, z = dp // NZ, lax.rem(dp, NZ)
@@ -147,29 +155,44 @@
         return 0
 
     lax.fori_loop(0, 64, arrange, 0, unroll=4)
-    own_facts = pltpu.make_async_copy(
-        table_ref.at[:, pl.ds(pl.multiple_of(z * 128, 128), 128)], facts.at[0], load_sem.at[3]
+    tables = ((plan_marks, facts), (plan_spots, spots))
+    own_tables = [
+        pltpu.make_async_copy(table.at[z], held.at[0], load_sem.at[3 + i])
+        for i, (table, held) in enumerate(tables)
+    ]
+    for copy in own_tables:
+        copy.start()
+    pl.semaphore_wait(barrier, 23)
+
+    def parts(ref, number, last):
+        return [ref.at[pl.ds(low, high - low)] for low, high in PIECES[number][:last]]
+
+    arrivals = (
+        {
+            1: parts(up_1, 1, 4),
+            2: [*parts(up_2a, 2, 3), up_2b],
+            3: (up_3a, up_3b, up_3c, up_3d),
+            4: (up_4a, up_4b),
+        },
+        {
+            1: parts(down_1, 1, 4),
+            2: [*parts(down_2a, 2, 3), down_2b],
+            3: (down_3a, down_3b, down_3c, down_3d),
+            4: (down_4a, down_4b),
+        },
     )
-    own_facts.start()
-    pl.semaphore_wait(barrier, 23)
-
-    def whole(ref, number):
-        return [ref.at[pl.ds(low, high - low)] for low, high in PIECES[number]]
-
-    thirds = ((up_3a, up_3b, up_3c, up_3d), (down_3a, down_3b, down_3c, down_3d))
-    arrivals = (
-        {1: whole(up_1, 1), 2: whole(up_2, 2), 3: thirds[0], 4: (up_4,)},
-        {1: whole(down_1, 1), 2: whole(down_2, 2), 3: thirds[1], 4: (down_4,)},
+    sources = (
+        {1: send_up, 2: up_1, 3: up_2a, 4: up_3a},
+        {1: send_down, 2: down_1, 3: down_2a, 4: down_3a},
     )
+    joints = ({2: up_2, 3: up_3, 4: up_4}, {2: down_2, 3: down_3, 4: down_4})
     targets = (at_plane(lax.rem(z + 1, NZ)), at_plane(lax.rem(z + NZ - 1, NZ)))
-    sources = ({1: send_up, 2: up_1, 3: up_2}, {1: send_down, 2: down_1, 3: down_2})
     ring_copies = {}
 
     def hop(way, number, piece):
         low, high = PIECES[number][piece]
-        src = thirds[way][0] if number == 4 else sources[way][number]
         copy = pltpu.make_async_remote_copy(
-            src_ref=src.at[pl.ds(low, high - low)],
+            src_ref=sources[way][number].at[pl.ds(low, high - low)],
             dst_ref=arrivals[way][number][piece],
             send_sem=ring_send.at[way, number - 1, piece],
             recv_sem=ring_recv.at[way, number - 1, piece],
@@ -179,21 +202,26 @@
         copy.start()
         ring_copies[way, number, piece] = copy
 
+    def join(way, number, piece):
+        low, high = PIECES[number][piece]
+        joints[way][number][pl.ds(low, high - low)] = arrivals[way][number][piece][...]
+
     fact_copies = []
     for d in range(1, NZ):
         z_to = lax.rem(z + d, NZ)
-        copy = pltpu.make_async_remote_copy(
-            src_ref=table_ref.at[:, pl.ds(pl.multiple_of(z_to * 128, 128), 128)],
-            dst_ref=facts.at[STEP_OF[d]],
-            send_sem=fact_send.at[d],
-            recv_sem=fact_recv.at[STEP_OF[d]],
-            device_id=at_plane(z_to),
-            device_id_type=MESH,
-        )
-        copy.start()
-        fact_copies.append(copy)
-
-    for piece in range(3):
+        for i, (table, held) in enumerate(tables):
+            copy = pltpu.make_async_remote_copy(
+                src_ref=table.at[z_to],
+                dst_ref=held.at[STEP_OF[d]],
+                send_sem=fact_send.at[i, d],
+                recv_sem=fact_recv.at[i, STEP_OF[d]],
+                device_id=at_plane(z_to),
+                device_id_type=MESH,
+            )
+            copy.start()
+            fact_copies.append(copy)
+
+    for piece in range(4):
         for way in range(2):
             hop(way, 1, piece)
 
@@ -246,13 +274,14 @@
 
     def forward(step):
         rows = got[step].reshape(256, feature)
+        turned[...] = rows.T
         pre_ref[...] = jnp.dot(rows, w_ref[...], preferred_element_type=f32) + bias_ref[...].astype(f32)
-        turned[...] = rows.T
         lanes = lax.broadcasted_iota(jnp.int32, (128, 128), 1)
+        every = marks[...].astype(f32)
         for k in range(2):
-            every = marks[:, 8 * k : 8 * k + 8].astype(f32).reshape(128, 128)
-            picked_marks = jnp.where(lanes == me + 16 * step, every, 0.0)
-            mark_col[pl.ds(128 * k, 128)] = jnp.sum(picked_marks, axis=1, keepdims=True)
+            mine = every[:, 8 * k : 8 * k + 8].reshape(128, 128)
+            mine = jnp.where(lanes == me + 16 * step, mine, 0.0)
+            mark_col[pl.ds(128 * k, 128)] = jnp.sum(mine, axis=1, keepdims=True)
 
         out_w = out_w_ref[...].astype(f32)
 
@@ -274,15 +303,12 @@
 
         lax.fori_loop(0, 16, group, 0, unroll=4)
 
-    def gradient(low, rows):
-        at = pl.ds(pl.multiple_of(low, 16), rows)
-        total[at] += jnp.dot(turned[at], low_ref[...], preferred_element_type=f32)
-
     def learn(step, _):
         received(step)
         forward(step)
         for i in range(2):
-            gradient(i * half, half)
+            at = pl.ds(i * half, half)
+            total[at] += jnp.dot(turned[at], low_ref[...], preferred_element_type=f32)
         return 0
 
     total[...] = jnp.zeros_like(total)
@@ -290,17 +316,18 @@
 
     for copy in fact_copies:
         copy.wait()
-    own_facts.wait()
+    for copy in own_tables:
+        copy.wait()
     place_copies = []
     for step in range(NZ):
         copy = pltpu.make_async_copy(
-            facts.at[step, pl.ds(16, 8)], places.at[step], place_sem.at[step]
+            spots.at[step], places.at[step], place_sem.at[step]
         )
         copy.start()
         place_copies.append(copy)
-    joined = facts[0, 0:16]
+    joined = facts[0]
     for step in range(1, NZ):
-        joined = joined + facts[step, 0:16]
+        joined = joined + facts[step]
     own_marks[...] = joined
     for copy in place_copies:
         copy.wait()
@@ -323,7 +350,7 @@
     for load in loads:
         load.wait()
 
-    for piece in range(3):
+    for piece in range(4):
         for way in range(2):
             ring_copies[way, 1, piece].wait_recv()
             hop(way, 2, piece)
@@ -333,9 +360,9 @@
     spread(2, 0, 4)
     most_marks = marks.at[pl.ds(0, 15)]
     pltpu.make_async_copy(most_marks, most_marks, mark_recv).wait()
-    lax.fori_loop(0, 1, learn, 0)
-
-    for piece in range(3):
+    lax.fori_loop(0, 3, learn, 0)
+
+    for piece in range(4):
         for way in range(2):
             ring_copies[way, 2, piece].wait_recv()
             if piece == 0:
@@ -343,39 +370,47 @@
             elif piece == 1:
                 for part in (1, 2, 3):
                     hop(way, 3, part)
-    pick(3, up_2, 0, 4)
-    pick(4, down_2, 0, 4)
-    spread(3, 0, 4)
-    spread(4, 0, 4)
-    lax.fori_loop(1, 3, learn, 0)
+        for way in range(2):
+            join(way, 2, piece)
+        if piece >= 2:
+            first, last = ((0, 1), (1, 4))[piece - 2]
+            for way in range(2):
+                pick(3 + way, joints[way][2], first, last)
+            spread(3, first, last)
+            spread(4, first, last)
 
     for kind in range(4):
-        low, high = PIECES[3][kind]
-        for way, joint in enumerate((up_3, down_3)):
+        for way in range(2):
             ring_copies[way, 3, kind].wait_recv()
             if kind == 0:
                 hop(way, 4, 0)
-            joint[pl.ds(low, high - low)] = thirds[way][kind][...]
-            pick(5 + way, joint, kind, kind + 1)
+                hop(way, 4, 1)
+        for way in range(2):
+            join(way, 3, kind)
+            pick(5 + way, joints[way][3], kind, kind + 1)
         spread(5, kind, kind + 1)
         spread(6, kind, kind + 1)
-    lax.fori_loop(3, 5, learn, 0)
-
-    for way, source in enumerate((up_4, down_4)):
-        ring_copies[way, 4, 0].wait_recv()
-        pick(7, source, 2 * way, 2 * way + 2)
-    spread(7, 0, 4)
+        if kind < 2:
+            lax.fori_loop(3 + kind, 4 + kind, learn, 0)
+
+    for piece in range(2):
+        for way in range(2):
+            ring_copies[way, 4, piece].wait_recv()
+            join(way, 4, piece)
+            kind = 2 * way + piece
+            pick(7, joints[way][4], kind, kind + 1)
+        for way in range(2):
+            kind = 2 * way + piece
+            spread(7, kind, kind + 1)
     lax.fori_loop(5, 7, learn, 0)
-    received(7)
-    forward(7)
 
     ours = core * half
     theirs = half - ours
 
-    def swap(i):
+    def to_partner(src, dst, i):
         copy = pltpu.make_async_remote_copy(
-            src_ref=total.at[pl.ds(pl.multiple_of(theirs + i * piece_rows, 16), piece_rows)],
-            dst_ref=other.at[pl.ds(i * piece_rows, piece_rows)],
+            src_ref=src,
+            dst_ref=dst,
             send_sem=swap_send.at[i],
             recv_sem=swap_recv.at[i],
             device_id=partner,
@@ -384,18 +419,15 @@
         copy.start()
         return copy
 
-    gradient(theirs, half)
-    swaps = [swap(0), swap(1)]
-    vec_swap = pltpu.make_async_remote_copy(
-        src_ref=vec_total,
-        dst_ref=vec_other,
-        send_sem=swap_send.at[2],
-        recv_sem=swap_recv.at[2],
-        device_id=partner,
-        device_id_type=MESH,
-    )
-    vec_swap.start()
-    gradient(ours, half)
+    our_half = pl.ds(pl.multiple_of(ours, 16), half)
+    their_half = pl.ds(pl.multiple_of(theirs, 16), half)
+    swaps = [to_partner(total.at[their_half], other, 0)]
+    received(7)
+    forward(7)
+    swaps.append(to_partner(turned.at[their_half], turned_other, 1))
+    swaps.append(to_partner(low_ref, low_other, 2))
+    vec_swap = to_partner(vec_total, vec_other, 3)
+    total[our_half] += jnp.dot(turned[our_half], low_ref[...], preferred_element_type=f32)
 
     vec_swap.wait_recv()
     vec_sum = vec_total[...] + vec_other[...]
@@ -409,9 +441,11 @@
         vector - learn_rate * new_first_vec / (jnp.sqrt(new_second_vec) + epsilon)
     ).astype(jnp.bfloat16)
 
+    for copy in swaps:
+        copy.wait_recv()
+    total[our_half] += jnp.dot(turned_other[...], low_other[...], preferred_element_type=f32)
     copies = []
     for i in range(2):
-        swaps[i].wait_recv()
 
         def adam(r, _):
             here = pl.multiple_of(i * piece_rows + r * 16, 16)
@@ -422,31 +456,14 @@
             second = beta_two * second_ref[at] + (1.0 - beta_two) * grad * grad
             new_first[at] = first
             new_second[at] = second
-            new_w[at] = (
+            new_w[there] = (
                 w_ref[there].astype(f32) - learn_rate * first / (jnp.sqrt(second) + epsilon)
             ).astype(jnp.bfloat16)
             return 0
 
         lax.fori_loop(0, piece_rows // 16, adam, 0, unroll=3)
-        at = pl.ds(i * piece_rows, piece_rows)
         there = pl.ds(pl.multiple_of(ours + i * piece_rows, 16), piece_rows)
-        for k, (src, dst) in enumerate(((new_first, new_first_hbm), (new_second, new_second_hbm))):
-            copy = pltpu.make_async_copy(src.at[at], dst.at[at], out_sem.at[k, i])
-            copy.start()
-            copies.append(copy)
-        copy = pltpu.make_async_remote_copy(
-            src_ref=new_w.at[at],
-            dst_ref=new_w_hbm.at[there],
-            send_sem=swap_send.at[3 + i],
-            recv_sem=swap_recv.at[3 + i],
-            device_id=partner,
-            device_id_type=MESH,
-        )
-        copy.start()
-        copies.append(copy)
-        copy = pltpu.make_async_copy(new_w.at[at], new_w_hbm.at[there], out_sem.at[2, i])
-        copy.start()
-        copies.append(copy)
+        copies.append(to_partner(new_w.at[there], new_w.at[there], 4 + i))
 
     vec_swap.wait_send()
     for copy in swaps:
@@ -461,6 +478,18 @@
         copy.wait()
 
 
+def write_kernel(*refs):
+    held, placed, sem = refs[:6], refs[6:12], refs[12]
+    copies = [
+        pltpu.make_async_copy(src, dst, sem.at[i])
+        for i, (src, dst) in enumerate(zip(held, placed, strict=True))
+    ]
+    for copy in copies:
+        copy.start()
+    for copy in copies:
+        copy.wait()
+
+
 def per_device(
     embeddings, coverage, labels, w_in, bias_in, w_out, first_w, second_w, first_vec, second_vec
 ):
@@ -472,77 +501,87 @@
     smem_in = pl.BlockSpec(memory_space=pltpu.SMEM)
     vmem_in = pl.BlockSpec(memory_space=vmem)
     any_in = pl.BlockSpec(memory_space=pl.ANY)
-    order, table = pl.pallas_call(
+    order, table_marks, table_spots = pl.pallas_call(
         plan_kernel,
         out_shape=(
             jax.ShapeDtypeStruct((2, 64), i32),
-            jax.ShapeDtypeStruct((24, NZ * 128), i32),
+            jax.ShapeDtypeStruct((NZ, 16, 128), bf16),
+            jax.ShapeDtypeStruct((NZ, 2, 128), i32),
         ),
         in_specs=[vmem_in] * 2,
-        out_specs=(vmem_in, vmem_in),
+        out_specs=[vmem_in] * 3,
         name="plan",
     )(coverage.T, labels.transpose(1, 2, 0))
-    new_vec, new_first_vec, new_second_vec, new_w, new_first, new_second = pl.pallas_call(
+    results = (
+        ((2, hid), bf16),
+        ((2, hid), f32),
+        ((2, hid), f32),
+        ((feature, hid), bf16),
+        ((half, hid), f32),
+        ((half, hid), f32),
+    )
+    made = pl.pallas_call(
         step_kernel,
-        out_shape=(
-            jax.ShapeDtypeStruct((2, hid), bf16),
-            jax.ShapeDtypeStruct((2, hid), f32),
-            jax.ShapeDtypeStruct((2, hid), f32),
-            jax.ShapeDtypeStruct((feature, hid), bf16),
-            jax.ShapeDtypeStruct((half, hid), f32),
-            jax.ShapeDtypeStruct((half, hid), f32),
-        ),
-        in_specs=[smem_in, *[vmem_in] * 6, *[any_in] * 3],
-        out_specs=(*[vmem_in] * 3, *[any_in] * 3),
+        out_shape=[vmem(shape, kind) for shape, kind in results],
+        in_specs=[smem_in, *[vmem_in] * 7, *[any_in] * 3],
+        out_specs=[vmem_in] * 6,
         scratch_shapes=[
             vmem((64, 8, feature), bf16),
             vmem((64, 8, feature), bf16),
-            *[vmem((size, 8, feature), bf16) for size in (64, 64, 24, 8, 8, 8, 16) * 2],
-            vmem((48, 8, feature), bf16),
-            vmem((48, 8, feature), bf16),
+            *[vmem((size, 8, feature), bf16) for size in (64, 56, 8, 24, 8, 8, 8, 8, 8) * 2],
+            *[vmem((size, 8, feature), bf16) for size in (64, 48, 16) * 2],
             vmem((NZ, 2, 16, 8, feature), bf16),
             vmem((NZ, 2, 16, 8, feature), bf16),
-            vmem((NZ, 24, 128), i32),
-            vmem((16, 128), i32),
-            vmem((16, 16, 128), i32),
+            vmem((NZ, 16, 128), bf16),
+            vmem((NZ, 2, 128), i32),
+            vmem((16, 128), bf16),
+            vmem((16, 16, 128), bf16),
             vmem((feature, hid), bf16),
             vmem((half, hid), f32),
             vmem((half, hid), f32),
-            vmem((half, hid), f32),
-            vmem((half, hid), f32),
-            vmem((half, hid), bf16),
             vmem((256, hid), f32),
             vmem((256, hid), bf16),
+            vmem((256, hid), bf16),
             vmem((feature, 256), bf16),
+            vmem((half, 256), bf16),
             vmem((feature, hid), f32),
             vmem((half, hid), f32),
             vmem((2, 8, hid), f32),
             vmem((2, 8, hid), f32),
             vmem((256, 1), f32),
-            pltpu.SMEM((NZ, 8, 128), i32),
+            pltpu.SMEM((NZ, 2, 128), i32),
             dma((2, 4, 4)),
             dma((2, 4, 4)),
-            dma((NZ,)),
-            dma((NZ,)),
+            dma((2, NZ)),
+            dma((2, NZ)),
             dma((NZ,)),
             dma((NZ,)),
             dma,
             dma,
             dma((NZ,)),
             dma((NZ,)),
-            dma((4,)),
             dma((5,)),
-            dma((5,)),
-            dma((3, 2)),
+            dma((6,)),
+            dma((6,)),
         ],
         compiler_params=pltpu.CompilerParams(
-            collective_id=0, has_side_effects=True, vmem_limit_bytes=60 << 20
+            collective_id=0, has_side_effects=True, vmem_limit_bytes=50 << 20
         ),
         name="adam_step",
     )(
-        order, table, embeddings, bias_in, w_out, first_vec[0], second_vec[0],
+        order, table_marks, table_spots, embeddings, bias_in, w_out, first_vec[0], second_vec[0],
         w_in[0], first_w[0], second_w[0],
     )
+    made = [pltpu.with_memory_space_constraint(array, vmem) for array in made]
+    new_vec, new_first_vec, new_second_vec, new_w, new_first, new_second = pl.pallas_call(
+        write_kernel,
+        out_shape=[jax.ShapeDtypeStruct(shape, kind) for shape, kind in results],
+        in_specs=[vmem_in] * 6,
+        out_specs=[any_in] * 6,
+        scratch_shapes=[dma((6,))],
+        compiler_params=pltpu.CompilerParams(vmem_limit_bytes=2 << 20),
+        name="write",
+    )(*made)
     return (
         new_w[None],
         new_vec[None],

time: 131 us -> 123 us (0.939)
  local copies, waits for them, and re-layouts: 8.03 us -> 0 us
    unnamed x16 -> x0, local copies, waits for them, and re-layouts: 8.03 us -> none
    pallas_call x1 -> x2, Pallas kernels: 120 us -> 121 us  [the longest x1 118 us: per_device(): pl.pallas_call(step_kernel, out_shape=[vmem(shape, kind) for shape, kind...]
where the time goes in v4:
time: 123 us
  Pallas kernels  122 us (99%)
    pallas_call x1, Pallas kernels, per_device(): pl.pallas_call(step_kernel, out_shape=[vmem(shape, kind) for shape, kind...  118 us

profile of v4, /device:TPU:25, one launch (start us, length us, event | category | flops | bytes accessed | tf_op | source)
XLA Modules:
  0.0 123.0 jit_solution(12280748732679795647)
XLA Ops:
  0.6 1.6 %plan.1 = (s32[2,64]{1,0:T(2,128)}, bf16[8,16,128]{2,1,0:T(8,128)(2,1)}, s32[8,2,128]{2,1,0:T(2,128)}) custom-call(s32[2,64]{1,0:T(2,128)} %bitcast.19, s32[2,8,64]{2,1,0:T(8,128)} %bitcast.16), custom_call_target="tpu_custom_call" | custom-call | tf_op jit(solution)/shard_map/plan/pallas_call | solution.py:504
  2.3 118.3 %adam_step.1 = (bf16[2,768]{1,0:T(2,128)(2,1)S(1)}, f32[2,768]{1,0:T(2,128)S(1)}, f32[2,768]{1,0:T(2,128)S(1)}, bf16[1152,768]{1,0:T(8,128)(2,1)S(1)}, f32[576,768]{1,0:T(8,128)S(1)}, /*index=5*/f32[576,768]{1,0:T(8,128)S(1)}) custom-call(s32[2,64]{1,0:T(2,128)} %get-tuple-element.21.order_ref, bf16[8,16,128]{2,1,0:T(8,128)(2,1)} %get-tuple-element.22.plan_marks, ...), custom_call_target="tpu_custom_call" | custom-call | tf_op jit(solution)/shard_map/adam_step/pallas_call | solution.py:523
  120.6 2.4 %write.1 = (bf16[2,768]{1,0:T(2,128)(2,1)}, f32[2,768]{1,0:T(2,128)}, f32[2,768]{1,0:T(2,128)}, bf16[1152,768]{1,0:T(8,128)(2,1)}, f32[576,768]{1,0:T(8,128)}, /*index=5*/f32[576,768]{1,0:T(8,128)}) custom-call(bf16[2,768]{1,0:T(2,128)(2,1)S(1)} %get-tuple-element.24.refs_0_, f32[2,768]{1,0:T(2,128)S(1)} %get-tuple-element.25.refs_1_, ...), custom_call_target="tpu_custom_call" | custom-call | tf_op jit(solution)/shard_map/write/pallas_call | solution.py:576

commit v5 on v4

--- a/solution.py
+++ b/solution.py
@@ -14,8 +14,8 @@
 NZ = 8
 STEP_OF = (0, 1, 3, 5, 7, 6, 4, 2)
 PIECES = {
-    1: ((0, 24), (24, 48), (48, 56), (56, 64)),
-    2: ((0, 24), (24, 48), (48, 56), (56, 64)),
+    1: ((0, 32), (32, 56), (56, 64)),
+    2: ((0, 32), (32, 56), (56, 64)),
     3: ((0, 24), (24, 32), (32, 40), (40, 48)),
     4: ((0, 8), (8, 16)),
 }
@@ -38,41 +38,45 @@
         return jnp.sum(jnp.where(flags, 1.0, 0.0), axis=0, keepdims=True).astype(i32)
 
     heads = [cover_ref[t : t + 1] for t in range(2)]
-    ahead, spot, up, far_up, far_down = [], [], [], None, None
+    ahead, spot, up, keys = [], [], [], [[], []]
     for head in heads:
         plane = (head >> 2) & 7
         x, y = head & 3, head >> 5
         kind = (x + y) & 3
         gap = (plane - z + NZ) & 7
         is_up = ((gap >= 1) & (gap <= 3)) | ((gap == 4) & (kind < 2))
-        is_down = (gap >= 5) | ((gap == 4) & (kind >= 2))
-        near = jnp.where(kind == 0, 4, 0)
-        rank_up = jnp.where(gap == 3, 8 - kind, jnp.where(gap == 2, near, 0))
-        rank_down = jnp.where(gap == 5, 8 - kind, jnp.where(gap == 6, near, 0))
-        rank_up = jnp.where(gap == 4, 10 - (kind & 1), rank_up)
-        rank_down = jnp.where(gap == 4, 10 - (kind & 1), rank_down)
-        rank_up = jnp.where(is_up, rank_up, 0)
-        rank_down = jnp.where(is_down, rank_down, 0)
-        far_up = rank_up if far_up is None else jnp.maximum(far_up, rank_up)
-        far_down = rank_down if far_down is None else jnp.maximum(far_down, rank_down)
+        for way in range(2):
+            hops = gap if way == 0 else NZ - gap
+            far = (gap == 4) & (is_up if way == 0 else ~is_up)
+            beyond = jnp.where(far, 10 - (kind & 1), jnp.where(hops == 3, 8 - kind, 0))
+            first = jnp.where(hops == 2, 20 - kind, jnp.where(far, 10, beyond))
+            keys[way].append((first, beyond))
         ahead.append(gap)
         spot.append(4 * kind + x)
         up.append(is_up)
 
-    places, orders = [], []
-    for far in (far_up, far_down):
-        tall = upright(far)
-        pos = count((tall > far) | ((tall == far) & (down_axis < along)))
+    wide = lax.broadcasted_iota(i32, (blocks, 128), 1)
+    earlier = down_axis < along
+    places, thirds, orders, relays = [], [], [], []
+    for way in range(2):
+        first, beyond = (jnp.maximum(keys[way][0][i], keys[way][1][i]) for i in range(2))
+        tall = upright(first)
+        pos = count((tall > first) | ((tall == first) & earlier))
+        tall_pos = upright(pos)
+        order = jnp.sum(jnp.where(tall_pos == along, down_axis, 0).astype(f32), axis=0, keepdims=True)
+        orders.append(order.astype(i32))
+        tall = upright(beyond)
+        same = count((tall == beyond) & earlier)
+        more = count(tall > beyond)
+        third = jnp.where(beyond >= 8, more + same, jnp.where(beyond > 0, 24 + 8 * (7 - beyond) + same, 99))
+        relay = jnp.where(upright(third) == wide, tall_pos, 0).astype(f32)
+        relays.append(jnp.sum(relay, axis=0, keepdims=True).astype(i32))
         places.append(pos)
-        order = jnp.sum(
-            jnp.where(upright(pos) == along, down_axis, 0).astype(f32), axis=0, keepdims=True
-        )
-        orders.append(order.astype(i32))
+        thirds.append(third)
     order_ref[0:1] = orders[0]
     order_ref[1:2] = orders[1]
 
     tall_heads = [upright(head) for head in heads]
-    earlier = down_axis < along
     ranks = [
         count((tall_heads[0] == heads[0]) & earlier),
         count(tall_heads[0] == heads[1]) + count((tall_heads[1] == heads[1]) & earlier),
@@ -85,7 +89,9 @@
         step = jnp.where(gap < 4, jnp.maximum(2 * gap - 1, 0), jnp.where(gap == 4, 7, 2 * (NZ - gap)))
         lane = plane * 128 + step * 16 + spot[t]
         picker = jnp.where(upright(lane) == lanes, 1.0, 0.0).astype(bf16)
-        pos = jnp.where(gap == 0, number, jnp.where(up[t], places[0], places[1]))
+        far = (gap >= 3) & (gap <= 5)
+        there = [jnp.where(far, thirds[way], places[way]) for way in range(2)]
+        pos = jnp.where(gap == 0, number, jnp.where(up[t], there[0], there[1]))
         mark = labels_ref[t] + 1
         rank = jnp.broadcast_to(ranks[t], (8, blocks))
         tall_pos = jnp.broadcast_to(pos, (8, blocks))
@@ -102,7 +108,10 @@
     for plane in range(NZ):
         part = table[:, plane * 128 : plane * 128 + 128]
         marks_ref[plane] = part[0:16].astype(bf16)
-        spots_ref[plane] = part[16:18].astype(i32)
+        gap = (plane - z + NZ) & 7
+        spots_ref[plane, 0:2] = part[16:18].astype(i32)
+        spots_ref[plane, 2:3] = jnp.where(gap == 2, relays[0], jnp.where(gap == 6, relays[1], 0))
+        spots_ref[plane, 3:4] = jnp.zeros((1, 128), i32)
 
 
 def step_kernel(
@@ -110,9 +119,9 @@
     w_hbm, first_hbm, second_hbm,
     new_vec_ref, new_first_vec_ref, new_second_vec_ref, new_w, new_first, new_second,
     send_up, send_down,
-    up_1, up_2a, up_2b, up_3a, up_3b, up_3c, up_3d, up_4a, up_4b,
-    down_1, down_2a, down_2b, down_3a, down_3b, down_3c, down_3d, down_4a, down_4b,
-    up_2, up_3, up_4, down_2, down_3, down_4,
+    up_1, up_2a, up_2b, up_2c, up_3a, up_3b, up_3c, up_3d, up_4a, up_4b,
+    down_1, down_2a, down_2b, down_2c, down_3a, down_3b, down_3c, down_3d, down_4a, down_4b,
+    up_2, up_3, up_4, up_next, down_2, down_3, down_4, down_next,
     picked, got, facts, spots, own_marks, marks, w_ref, first_ref, second_ref,
     pre_ref, low_ref, low_other, turned, turned_other, total, other, vec_total, vec_other,
     mark_col, places,
@@ -164,26 +173,26 @@
         copy.start()
     pl.semaphore_wait(barrier, 23)
 
-    def parts(ref, number, last):
-        return [ref.at[pl.ds(low, high - low)] for low, high in PIECES[number][:last]]
+    def parts(ref, number):
+        return [ref.at[pl.ds(low, high - low)] for low, high in PIECES[number]]
 
     arrivals = (
         {
-            1: parts(up_1, 1, 4),
-            2: [*parts(up_2a, 2, 3), up_2b],
+            1: parts(up_1, 1),
+            2: (up_2a, up_2b, up_2c),
             3: (up_3a, up_3b, up_3c, up_3d),
             4: (up_4a, up_4b),
         },
         {
-            1: parts(down_1, 1, 4),
-            2: [*parts(down_2a, 2, 3), down_2b],
+            1: parts(down_1, 1),
+            2: (down_2a, down_2b, down_2c),
             3: (down_3a, down_3b, down_3c, down_3d),
             4: (down_4a, down_4b),
         },
     )
     sources = (
-        {1: send_up, 2: up_1, 3: up_2a, 4: up_3a},
-        {1: send_down, 2: down_1, 3: down_2a, 4: down_3a},
+        {1: send_up, 2: up_1, 3: up_next, 4: up_3a},
+        {1: send_down, 2: down_1, 3: down_next, 4: down_3a},
     )
     joints = ({2: up_2, 3: up_3, 4: up_4}, {2: down_2, 3: down_3, 4: down_4})
     targets = (at_plane(lax.rem(z + 1, NZ)), at_plane(lax.rem(z + NZ - 1, NZ)))
@@ -221,7 +230,7 @@
             copy.start()
             fact_copies.append(copy)
 
-    for piece in range(4):
+    for piece in range(3):
         for way in range(2):
             hop(way, 1, piece)
 
@@ -350,7 +359,14 @@
     for load in loads:
         load.wait()
 
-    for piece in range(4):
+    def relay(way, low, high):
+        def one(i, _):
+            sources[way][3][i] = joints[way][2][places[3 + way, 2, i]]
+            return 0
+
+        lax.fori_loop(low, high, one, 0, unroll=4)
+
+    for piece in range(3):
         for way in range(2):
             ring_copies[way, 1, piece].wait_recv()
             hop(way, 2, piece)
@@ -360,24 +376,31 @@
     spread(2, 0, 4)
     most_marks = marks.at[pl.ds(0, 15)]
     pltpu.make_async_copy(most_marks, most_marks, mark_recv).wait()
-    lax.fori_loop(0, 3, learn, 0)
-
-    for piece in range(4):
-        for way in range(2):
-            ring_copies[way, 2, piece].wait_recv()
-            if piece == 0:
-                hop(way, 3, 0)
-            elif piece == 1:
-                for part in (1, 2, 3):
-                    hop(way, 3, part)
-        for way in range(2):
-            join(way, 2, piece)
-        if piece >= 2:
-            first, last = ((0, 1), (1, 4))[piece - 2]
-            for way in range(2):
-                pick(3 + way, joints[way][2], first, last)
-            spread(3, first, last)
-            spread(4, first, last)
+    lax.fori_loop(0, 1, learn, 0)
+
+    for way, source in enumerate((up_2a, down_2a)):
+        ring_copies[way, 2, 0].wait_recv()
+        pick(3 + way, source, 0, 4)
+    spread(3, 0, 4)
+    spread(4, 0, 4)
+    for way in range(2):
+        join(way, 2, 0)
+    lax.fori_loop(1, 2, learn, 0)
+
+    for way in range(2):
+        ring_copies[way, 2, 1].wait_recv()
+        join(way, 2, 1)
+        relay(way, 0, 24)
+    for way in range(2):
+        hop(way, 3, 0)
+    for way in range(2):
+        ring_copies[way, 2, 2].wait_recv()
+        join(way, 2, 2)
+        relay(way, 24, 48)
+    for way in range(2):
+        for piece in (1, 2, 3):
+            hop(way, 3, piece)
+    lax.fori_loop(2, 5, learn, 0)
 
     for kind in range(4):
         for way in range(2):
@@ -390,8 +413,6 @@
             pick(5 + way, joints[way][3], kind, kind + 1)
         spread(5, kind, kind + 1)
         spread(6, kind, kind + 1)
-        if kind < 2:
-            lax.fori_loop(3 + kind, 4 + kind, learn, 0)
 
     for piece in range(2):
         for way in range(2):
@@ -506,7 +527,7 @@
         out_shape=(
             jax.ShapeDtypeStruct((2, 64), i32),
             jax.ShapeDtypeStruct((NZ, 16, 128), bf16),
-            jax.ShapeDtypeStruct((NZ, 2, 128), i32),
+            jax.ShapeDtypeStruct((NZ, 4, 128), i32),
         ),
         in_specs=[vmem_in] * 2,
         out_specs=[vmem_in] * 3,
@@ -528,12 +549,12 @@
         scratch_shapes=[
             vmem((64, 8, feature), bf16),
             vmem((64, 8, feature), bf16),
-            *[vmem((size, 8, feature), bf16) for size in (64, 56, 8, 24, 8, 8, 8, 8, 8) * 2],
-            *[vmem((size, 8, feature), bf16) for size in (64, 48, 16) * 2],
+            *[vmem((size, 8, feature), bf16) for size in (64, 32, 24, 8, 24, 8, 8, 8, 8, 8) * 2],
+            *[vmem((size, 8, feature), bf16) for size in (64, 48, 16, 48) * 2],
             vmem((NZ, 2, 16, 8, feature), bf16),
             vmem((NZ, 2, 16, 8, feature), bf16),
             vmem((NZ, 16, 128), bf16),
-            vmem((NZ, 2, 128), i32),
+            vmem((NZ, 4, 128), i32),
             vmem((16, 128), bf16),
             vmem((16, 16, 128), bf16),
             vmem((feature, hid), bf16),
@@ -549,7 +570,7 @@
             vmem((2, 8, hid), f32),
             vmem((2, 8, hid), f32),
             vmem((256, 1), f32),
-            pltpu.SMEM((NZ, 2, 128), i32),
+            pltpu.SMEM((NZ, 4, 128), i32),
             dma((2, 4, 4)),
             dma((2, 4, 4)),
             dma((2, NZ)),

time: 123 us -> 122 us (level)
  no operation moved by 1% of the time
where the time goes in v5:
time: 122 us
  Pallas kernels  121 us (99%)
    pallas_call x1, Pallas kernels, per_device(): pl.pallas_call(step_kernel, out_shape=[vmem(shape, kind) for shape, kind...  117 us

profile of v5, /device:TPU:25, one launch (start us, length us, event | category | flops | bytes accessed | tf_op | source)
XLA Modules:
  0.0 122.0 jit_solution(5848072127499536286)
XLA Ops:
  0.6 1.7 %plan.1 = (s32[2,64]{1,0:T(2,128)}, bf16[8,16,128]{2,1,0:T(8,128)(2,1)}, s32[8,4,128]{2,1,0:T(4,128)}) custom-call(s32[2,64]{1,0:T(2,128)} %bitcast.19, s32[2,8,64]{2,1,0:T(8,128)} %bitcast.16), custom_call_target="tpu_custom_call" | custom-call | tf_op jit(solution)/shard_map/plan/pallas_call | solution.py:525
  2.3 117.2 %adam_step.1 = (bf16[2,768]{1,0:T(2,128)(2,1)S(1)}, f32[2,768]{1,0:T(2,128)S(1)}, f32[2,768]{1,0:T(2,128)S(1)}, bf16[1152,768]{1,0:T(8,128)(2,1)S(1)}, f32[576,768]{1,0:T(8,128)S(1)}, /*index=5*/f32[576,768]{1,0:T(8,128)S(1)}) custom-call(s32[2,64]{1,0:T(2,128)} %get-tuple-element.21.order_ref, bf16[8,16,128]{2,1,0:T(8,128)(2,1)} %get-tuple-element.22.plan_marks, ...), custom_call_target="tpu_custom_call" | custom-call | tf_op jit(solution)/shard_map/adam_step/pallas_call | solution.py:544
  119.5 2.4 %write.1 = (bf16[2,768]{1,0:T(2,128)(2,1)}, f32[2,768]{1,0:T(2,128)}, f32[2,768]{1,0:T(2,128)}, bf16[1152,768]{1,0:T(8,128)(2,1)}, f32[576,768]{1,0:T(8,128)}, /*index=5*/f32[576,768]{1,0:T(8,128)}) custom-call(bf16[2,768]{1,0:T(2,128)(2,1)S(1)} %get-tuple-element.24.refs_0_, f32[2,768]{1,0:T(2,128)S(1)} %get-tuple-element.25.refs_1_, ...), custom_call_target="tpu_custom_call" | custom-call | tf_op jit(solution)/shard_map/write/pallas_call | solution.py:597

commit v6 on v5

--- a/solution.py
+++ b/solution.py
@@ -115,10 +115,10 @@
 
 
 def step_kernel(
-    order_ref, plan_marks, plan_spots, emb_ref, bias_ref, out_w_ref, first_vec_ref, second_vec_ref,
+    order_ref, plan_marks, plan_spots, emb_hbm, bias_ref, out_w_ref, first_vec_ref, second_vec_ref,
     w_hbm, first_hbm, second_hbm,
     new_vec_ref, new_first_vec_ref, new_second_vec_ref, new_w, new_first, new_second,
-    send_up, send_down,
+    emb_ref, send_up, send_down,
     up_1, up_2a, up_2b, up_2c, up_3a, up_3b, up_3c, up_3d, up_4a, up_4b,
     down_1, down_2a, down_2b, down_2c, down_3a, down_3b, down_3c, down_3d, down_4a, down_4b,
     up_2, up_3, up_4, up_next, down_2, down_3, down_4, down_next,
@@ -157,6 +157,10 @@
 
     lax.fori_loop(1, 16, greet, 0)
     pl.semaphore_signal(barrier, inc=1, device_id=partner, device_id_type=MESH)
+
+    emb_copy = pltpu.make_async_copy(emb_hbm, emb_ref, load_sem.at[5])
+    emb_copy.start()
+    emb_copy.wait()
 
     def arrange(i, _):
         send_up[i] = emb_ref[order_ref[0, i]]
@@ -230,10 +234,14 @@
             copy.start()
             fact_copies.append(copy)
 
-    for piece in range(3):
-        for way in range(2):
-            hop(way, 1, piece)
-
+    for way in range(2):
+        hop(way, 1, 0)
+
+    def gone(way, number, piece):
+        ring_copies[way, number, piece].wait_send()
+        left.add((way, number, piece))
+
+    left = set()
     loads = [
         pltpu.make_async_copy(src, dst, load_sem.at[i])
         for i, (src, dst) in enumerate(
@@ -275,6 +283,10 @@
             return 0
 
         lax.fori_loop(4 * first, 4 * last, send, 0)
+
+    def sent(step):
+        most = got.at[step, :, pl.ds(0, 15)]
+        pltpu.make_async_copy(most, most, plane_send.at[step]).wait()
 
     def received(step):
         most = got.at[step, :, pl.ds(0, 15)]
@@ -310,7 +322,7 @@
             vec_total[1] += swing[0:8] + swing[8:16]
             return 0
 
-        lax.fori_loop(0, 16, group, 0, unroll=4)
+        lax.fori_loop(0, 16, group, 0, unroll=8)
 
     def learn(step, _):
         received(step)
@@ -366,18 +378,27 @@
 
         lax.fori_loop(low, high, one, 0, unroll=4)
 
-    for piece in range(3):
-        for way in range(2):
+    for way in range(2):
+        gone(way, 1, 0)
+        hop(way, 1, 1)
+    for way in range(2):
+        ring_copies[way, 1, 0].wait_recv()
+        gone(way, 1, 1)
+        hop(way, 1, 2)
+        hop(way, 2, 0)
+    for way, source in enumerate((up_1, down_1)):
+        for piece in (1, 2):
             ring_copies[way, 1, piece].wait_recv()
-            hop(way, 2, piece)
-    pick(1, up_1, 0, 4)
-    pick(2, down_1, 0, 4)
+        pick(1 + way, source, 0, 4)
     spread(1, 0, 4)
     spread(2, 0, 4)
     most_marks = marks.at[pl.ds(0, 15)]
     pltpu.make_async_copy(most_marks, most_marks, mark_recv).wait()
     lax.fori_loop(0, 1, learn, 0)
 
+    for way in range(2):
+        gone(way, 2, 0)
+        hop(way, 2, 1)
     for way, source in enumerate((up_2a, down_2a)):
         ring_copies[way, 2, 0].wait_recv()
         pick(3 + way, source, 0, 4)
@@ -385,8 +406,9 @@
     spread(4, 0, 4)
     for way in range(2):
         join(way, 2, 0)
-    lax.fori_loop(1, 2, learn, 0)
-
+    for way in range(2):
+        gone(way, 2, 1)
+        hop(way, 2, 2)
     for way in range(2):
         ring_copies[way, 2, 1].wait_recv()
         join(way, 2, 1)
@@ -397,22 +419,30 @@
         ring_copies[way, 2, 2].wait_recv()
         join(way, 2, 2)
         relay(way, 24, 48)
-    for way in range(2):
-        for piece in (1, 2, 3):
-            hop(way, 3, piece)
-    lax.fori_loop(2, 5, learn, 0)
-
+    lax.fori_loop(1, 3, learn, 0)
+
+    for way in range(2):
+        gone(way, 3, 0)
+        hop(way, 3, 1)
     for kind in range(4):
         for way in range(2):
             ring_copies[way, 3, kind].wait_recv()
-            if kind == 0:
-                hop(way, 4, 0)
-                hop(way, 4, 1)
-        for way in range(2):
             join(way, 3, kind)
             pick(5 + way, joints[way][3], kind, kind + 1)
+        if kind == 0:
+            for way in range(2):
+                hop(way, 3, 2)
         spread(5, kind, kind + 1)
         spread(6, kind, kind + 1)
+        if kind == 0:
+            lax.fori_loop(3, 4, learn, 0)
+        if kind < 3:
+            number, piece = ((3, 3), (4, 0), (4, 1))[kind]
+            for way in range(2):
+                gone(way, 3, kind + 1)
+                hop(way, number, piece)
+        if kind == 2:
+            lax.fori_loop(4, 5, learn, 0)
 
     for piece in range(2):
         for way in range(2):
@@ -420,6 +450,9 @@
             join(way, 4, piece)
             kind = 2 * way + piece
             pick(7, joints[way][4], kind, kind + 1)
+        if piece == 0:
+            sent(5)
+            sent(6)
         for way in range(2):
             kind = 2 * way + piece
             spread(7, kind, kind + 1)
@@ -489,12 +522,12 @@
     vec_swap.wait_send()
     for copy in swaps:
         copy.wait_send()
-    for copy in ring_copies.values():
-        copy.wait_send()
+    for key, copy in ring_copies.items():
+        if key not in left:
+            copy.wait_send()
     pltpu.make_async_copy(most_marks, most_marks, mark_send).wait()
-    for step in range(NZ):
-        most = got.at[step, :, pl.ds(0, 15)]
-        pltpu.make_async_copy(most, most, plane_send.at[step]).wait()
+    for step in (0, 1, 2, 3, 4, 7):
+        sent(step)
     for copy in copies:
         copy.wait()
 
@@ -544,11 +577,10 @@
     made = pl.pallas_call(
         step_kernel,
         out_shape=[vmem(shape, kind) for shape, kind in results],
-        in_specs=[smem_in, *[vmem_in] * 7, *[any_in] * 3],
+        in_specs=[smem_in, *[vmem_in] * 2, any_in, *[vmem_in] * 4, *[any_in] * 3],
         out_specs=[vmem_in] * 6,
         scratch_shapes=[
-            vmem((64, 8, feature), bf16),
-            vmem((64, 8, feature), bf16),
+            *[vmem((64, 8, feature), bf16) for _ in range(3)],
             *[vmem((size, 8, feature), bf16) for size in (64, 32, 24, 8, 24, 8, 8, 8, 8, 8) * 2],
             *[vmem((size, 8, feature), bf16) for size in (64, 48, 16, 48) * 2],
             vmem((NZ, 2, 16, 8, feature), bf16),
@@ -581,7 +613,7 @@
             dma,
             dma((NZ,)),
             dma((NZ,)),
-            dma((5,)),
+            dma((6,)),
             dma((6,)),
             dma((6,)),
         ],

time: 122 us -> 119 us (0.975); the launches traced: 122 us -> 117 us
  Pallas kernels: 121 us -> 117 us
    pallas_call x1, Pallas kernels: 117 us -> 113 us  [per_device(): pl.pallas_call(step_kernel, out_shape=[vmem(shape, kind) for shape, kind...]
where the time goes in v6:
time: 119 us; the launch traced here: 117 us
  Pallas kernels  117 us (98%)
    pallas_call x1, Pallas kernels, per_device(): pl.pallas_call(step_kernel, out_shape=[vmem(shape, kind) for shape, kind...  113 us
    pallas_call x1, Pallas kernels, per_device(): pl.pallas_call(write_kernel, out_shape=[jax.ShapeDtypeStruct(shape, kind)...  2.44 us

profile of v6, /device:TPU:25, one launch (start us, length us, event | category | flops | bytes accessed | tf_op | source)
XLA Modules:
  0.0 117.3 jit_solution(263017264907987782)
XLA Ops:
  0.6 1.7 %plan.1 = (s32[2,64]{1,0:T(2,128)}, bf16[8,16,128]{2,1,0:T(8,128)(2,1)}, s32[8,4,128]{2,1,0:T(4,128)}) custom-call(s32[2,64]{1,0:T(2,128)} %bitcast.19, s32[2,8,64]{2,1,0:T(8,128)} %bitcast.16), custom_call_target="tpu_custom_call" | custom-call | tf_op jit(solution)/shard_map/plan/pallas_call | solution.py:558
  2.3 112.6 %adam_step.1 = (bf16[2,768]{1,0:T(2,128)(2,1)S(1)}, f32[2,768]{1,0:T(2,128)S(1)}, f32[2,768]{1,0:T(2,128)S(1)}, bf16[1152,768]{1,0:T(8,128)(2,1)S(1)}, f32[576,768]{1,0:T(8,128)S(1)}, /*index=5*/f32[576,768]{1,0:T(8,128)S(1)}) custom-call(s32[2,64]{1,0:T(2,128)} %get-tuple-element.21.order_ref, bf16[8,16,128]{2,1,0:T(8,128)(2,1)} %get-tuple-element.22.plan_marks, ...), custom_call_target="tpu_custom_call" | custom-call | tf_op jit(solution)/shard_map/adam_step/pallas_call | solution.py:577
  114.9 2.4 %write.1 = (bf16[2,768]{1,0:T(2,128)(2,1)}, f32[2,768]{1,0:T(2,128)}, f32[2,768]{1,0:T(2,128)}, bf16[1152,768]{1,0:T(8,128)(2,1)}, f32[576,768]{1,0:T(8,128)}, /*index=5*/f32[576,768]{1,0:T(8,128)}) custom-call(bf16[2,768]{1,0:T(2,128)(2,1)S(1)} %get-tuple-element.24.refs_0_, f32[2,768]{1,0:T(2,128)S(1)} %get-tuple-element.25.refs_1_, ...), custom_call_target="tpu_custom_call" | custom-call | tf_op jit(solution)/shard_map/write/pallas_call | solution.py:629

commit v7 on v6

--- a/solution.py
+++ b/solution.py
@@ -123,7 +123,7 @@
     down_1, down_2a, down_2b, down_2c, down_3a, down_3b, down_3c, down_3d, down_4a, down_4b,
     up_2, up_3, up_4, up_next, down_2, down_3, down_4, down_next,
     picked, got, facts, spots, own_marks, marks, w_ref, first_ref, second_ref,
-    pre_ref, low_ref, low_other, turned, turned_other, total, other, vec_total, vec_other,
+    pre_ref, low_ref, low_pair, low_other, turned, turned_pair, turned_other, total, other, vec_total, vec_other,
     mark_col, places,
     ring_send, ring_recv, fact_send, fact_recv, place_sem, own_sem,
     mark_send, mark_recv, plane_send, plane_recv, load_sem, swap_send, swap_recv,
@@ -293,16 +293,17 @@
         pltpu.make_async_copy(most, most, plane_recv.at[step]).wait()
         pltpu.make_async_copy(picked.at[step, :, me], got.at[step, :, me], own_sem.at[step]).wait()
 
-    def forward(step):
-        rows = got[step].reshape(256, feature)
+    def forward(step, turned, low_ref, pair=1):
+        rows = got[pl.ds(step, pair)].reshape(256 * pair, feature)
         turned[...] = rows.T
-        pre_ref[...] = jnp.dot(rows, w_ref[...], preferred_element_type=f32) + bias_ref[...].astype(f32)
+        pre_ref[pl.ds(0, 256 * pair)] = jnp.dot(rows, w_ref[...], preferred_element_type=f32) + bias_ref[...].astype(f32)
         lanes = lax.broadcasted_iota(jnp.int32, (128, 128), 1)
         every = marks[...].astype(f32)
-        for k in range(2):
+        for i in range(2 * pair):
+            k = i % 2
             mine = every[:, 8 * k : 8 * k + 8].reshape(128, 128)
-            mine = jnp.where(lanes == me + 16 * step, mine, 0.0)
-            mark_col[pl.ds(128 * k, 128)] = jnp.sum(mine, axis=1, keepdims=True)
+            mine = jnp.where(lanes == me + 16 * (step + i // 2), mine, 0.0)
+            mark_col[pl.ds(128 * i, 128)] = jnp.sum(mine, axis=1, keepdims=True)
 
         out_w = out_w_ref[...].astype(f32)
 
@@ -322,11 +323,11 @@
             vec_total[1] += swing[0:8] + swing[8:16]
             return 0
 
-        lax.fori_loop(0, 16, group, 0, unroll=8)
+        lax.fori_loop(0, 16 * pair, group, 0, unroll=8)
 
     def learn(step, _):
         received(step)
-        forward(step)
+        forward(step, turned, low_ref)
         for i in range(2):
             at = pl.ds(i * half, half)
             total[at] += jnp.dot(turned[at], low_ref[...], preferred_element_type=f32)
@@ -456,7 +457,9 @@
         for way in range(2):
             kind = 2 * way + piece
             spread(7, kind, kind + 1)
-    lax.fori_loop(5, 7, learn, 0)
+    received(5)
+    received(6)
+    forward(5, turned_pair, low_pair, 2)
 
     ours = core * half
     theirs = half - ours
@@ -475,9 +478,12 @@
 
     our_half = pl.ds(pl.multiple_of(ours, 16), half)
     their_half = pl.ds(pl.multiple_of(theirs, 16), half)
-    swaps = [to_partner(total.at[their_half], other, 0)]
+    for at in (their_half, our_half):
+        total[at] += jnp.dot(turned_pair[at], low_pair[...], preferred_element_type=f32)
+        if at is their_half:
+            swaps = [to_partner(total.at[their_half], other, 0)]
     received(7)
-    forward(7)
+    forward(7, turned, low_ref)
     swaps.append(to_partner(turned.at[their_half], turned_other, 1))
     swaps.append(to_partner(low_ref, low_other, 2))
     vec_swap = to_partner(vec_total, vec_other, 3)
@@ -592,16 +598,18 @@
             vmem((feature, hid), bf16),
             vmem((half, hid), f32),
             vmem((half, hid), f32),
-            vmem((256, hid), f32),
+            vmem((512, hid), f32),
             vmem((256, hid), bf16),
+            vmem((512, hid), bf16),
             vmem((256, hid), bf16),
             vmem((feature, 256), bf16),
+            vmem((feature, 512), bf16),
             vmem((half, 256), bf16),
             vmem((feature, hid), f32),
             vmem((half, hid), f32),
             vmem((2, 8, hid), f32),
             vmem((2, 8, hid), f32),
-            vmem((256, 1), f32),
+            vmem((512, 1), f32),
             pltpu.SMEM((NZ, 4, 128), i32),
             dma((2, 4, 4)),
             dma((2, 4, 4)),

time: 119 us -> 119 us (level)
  no operation moved by 1% of the time
where the time goes in v7:
time: 119 us; the launch traced here: 117 us
  Pallas kernels  116 us (97%)
    pallas_call x1, Pallas kernels, per_device(): pl.pallas_call(step_kernel, out_shape=[vmem(shape, kind) for shape, kind...  112 us
    pallas_call x1, Pallas kernels, per_device(): pl.pallas_call(write_kernel, out_shape=[jax.ShapeDtypeStruct(shape, kind)...  2.44 us

profile of v7, /device:TPU:25, one launch (start us, length us, event | category | flops | bytes accessed | tf_op | source)
XLA Modules:
  0.0 117.0 jit_solution(4768746865858380505)
XLA Ops:
  0.6 1.7 %plan.1 = (s32[2,64]{1,0:T(2,128)}, bf16[8,16,128]{2,1,0:T(8,128)(2,1)}, s32[8,4,128]{2,1,0:T(4,128)}) custom-call(s32[2,64]{1,0:T(2,128)} %bitcast.19, s32[2,8,64]{2,1,0:T(8,128)} %bitcast.16), custom_call_target="tpu_custom_call" | custom-call | tf_op jit(solution)/shard_map/plan/pallas_call | solution.py:564
  2.3 112.2 %adam_step.1 = (bf16[2,768]{1,0:T(2,128)(2,1)S(1)}, f32[2,768]{1,0:T(2,128)S(1)}, f32[2,768]{1,0:T(2,128)S(1)}, bf16[1152,768]{1,0:T(8,128)(2,1)S(1)}, f32[576,768]{1,0:T(8,128)S(1)}, /*index=5*/f32[576,768]{1,0:T(8,128)S(1)}) custom-call(s32[2,64]{1,0:T(2,128)} %get-tuple-element.21.order_ref, bf16[8,16,128]{2,1,0:T(8,128)(2,1)} %get-tuple-element.22.plan_marks, ...), custom_call_target="tpu_custom_call" | custom-call | tf_op jit(solution)/shard_map/adam_step/pallas_call | solution.py:583
  114.5 2.4 %write.1 = (bf16[2,768]{1,0:T(2,128)(2,1)}, f32[2,768]{1,0:T(2,128)}, f32[2,768]{1,0:T(2,128)}, bf16[1152,768]{1,0:T(8,128)(2,1)}, f32[576,768]{1,0:T(8,128)}, /*index=5*/f32[576,768]{1,0:T(8,128)}) custom-call(bf16[2,768]{1,0:T(2,128)(2,1)S(1)} %get-tuple-element.24.refs_0_, f32[2,768]{1,0:T(2,128)S(1)} %get-tuple-element.25.refs_1_, ...), custom_call_target="tpu_custom_call" | custom-call | tf_op jit(solution)/shard_map/write/pallas_call | solution.py:637
